TPU v7x, 1024 devices: a whole 4x4x32 slice. The times are simulated.
1024 devices in a mesh: section: 4 (over y), seq: 8 (over x, core), tp: 32 (over z).
Axes of the slice: x: 4, y: 4, z: 32, core: 2. Of those that a mesh axis runs over, the one named last changes fastest.
Arguments:
- waiting_batchlets: bfloat16 [4, 1024, 4096], P('section', 'seq', 'tp'), may hold values from -6 to 6
- arriving_batchlet: bfloat16 [1024, 4096], P('seq', 'tp'), may hold values from -6 to 6
- entry_rescale_factor: float32 [4, 4096], P('section'), may hold values from 0.25 to 1.75
- entry_projection_matrix: bfloat16 [4, 4096, 16384], P('section', None, 'tp'), may hold values from -0.09375 to 0.09375
- timescale_projection: bfloat16 [4, 4096, 128], P('section', None, 'tp'), may hold values from -0.09375 to 0.09375
- timescale_offset: float32 [4, 128], P('section', 'tp'), may hold values from -1 to 1
- channel_forgetting_rate: int32 [4, 128], P('section', 'tp'), may hold values from 0 to 7
- state_read_write_matrix: bfloat16 [4, 4096, 4096], P('section', None, 'tp'), may hold values from -0.0234375 to 0.0234375
- direct_passthrough: float32 [4, 128], P('section', 'tp'), may hold values from 0.5 to 1.5
- closing_rescale_factor: float32 [4, 8192], P('section', 'tp'), may hold values from 0.25 to 1.75
- closing_projection_matrix: bfloat16 [4, 8192, 4096], P('section', 'tp'), may hold values from -0.0625 to 0.0625
Outputs:
- section_out: bfloat16 [4, 1024, 4096], P('section', 'seq', 'tp')
All inputs are finite; a program needn't handle non-finite values.
Results may differ from a plain program's by a relative error of at most 0.03.
Values may be sent and summed in bfloat16 or wider, within the bound.
No kernel may reach another device: no remote copies, remote signals or barrier semaphores. Data moves between devices by JAX's collectives and lax.ppermute only.
A program may use at most 128 MiB of HBM per device.

v0:
```python
import jax
import jax.numpy as jnp
from jax import lax
from jax.sharding import Mesh
from jax.sharding import PartitionSpec as P

HIDDEN_DIMENSION = 4096
HEADS = 128
NGROUPS = 8
HEAD_DIM = 64
STATE = 256
SEQ = ("seq_0", "seq_1")


def copy_for_each(value, axis):
    peers = lax.axis_size(axis)
    return lax.all_to_all(
        jnp.broadcast_to(value[None], (peers, *value.shape)), axis, 0, 0, tiled=True
    )


def in_order(parts, dim):
    parts = jnp.moveaxis(parts, 0, dim)
    shape = parts.shape
    return parts.reshape(*shape[:dim], shape[dim] * shape[dim + 1], *shape[dim + 2 :])


def collect(value, axis, dim):
    parts = copy_for_each(value, axis)
    return in_order(parts, dim)


def cut_rows(length, count):
    unit = 8 if length >= 8 * count else 1
    return [length // unit * k // count * unit for k in range(1, count)]


def stacked_from(value, axes, turns):
    parts = value[None]
    for k in turns:
        parts = lax.all_gather(parts, axes[k], axis=0, tiled=True)
    current = [lax.axis_size(axes[k]) for k in reversed(turns)]
    parts = parts.reshape(*current, *value.shape)
    turned = sorted(range(len(turns)), key=lambda place: turns[len(turns) - 1 - place])
    return parts.transpose(*turned, *range(len(turns), parts.ndim)).reshape(-1, *value.shape)


def gather_at_once(value, axes, dim):
    numbers = list(range(len(axes)))[::-1]
    widest = value.shape.index(max(value.shape[:-1] or value.shape))
    edges = [0, *cut_rows(value.shape[widest], len(axes)), value.shape[widest]]
    finished = []
    for k, (start, end) in enumerate(zip(edges, edges[1:])):
        if end > start:
            share = lax.slice_in_dim(value, start, end, axis=widest)
            finished.append(stacked_from(share, axes, numbers[k:] + numbers[:k]))
    return in_order(jnp.concatenate(finished, axis=widest + 1), dim)


def taken_together(value, axis):
    return copy_for_each(value, axis).sum(axis=0)


def split_up(value, dim, peers):
    before, after = (value.shape[:dim], value.shape[dim + 1 :])
    return jnp.moveaxis(value.reshape(*before, peers, -1, *after), dim, 0)


def sum_at_owner(value, axis, dim):
    peers = lax.axis_size(axis)
    parts = lax.all_to_all(split_up(value, dim, peers), axis, 0, 0, tiled=True)
    return jnp.sum(parts.astype(jnp.float32), axis=0)


def shifted(block, axis, distance):
    devices = range(lax.axis_size(axis))
    route = [(i - distance, i) for i in devices if i - distance in devices]
    return lax.ppermute(block, axis, route)


def body(
    waiting_batchlets,
    arriving_batchlet,
    entry_rescale_factor,
    entry_projection_matrix,
    timescale_projection,
    timescale_offset,
    channel_forgetting_rate,
    state_read_write_matrix,
    direct_passthrough,
    closing_rescale_factor,
    closing_projection_matrix,
):
    gain = entry_rescale_factor[0]
    w_inp = entry_projection_matrix[0]
    w_step = timescale_projection[0]
    bias = timescale_offset[0]
    code = channel_forgetting_rate[0]
    w_shared = state_read_write_matrix[0]
    skip_coef = direct_passthrough[0]
    o_gain = closing_rescale_factor[0]
    w_outp = closing_projection_matrix[0]
    heads_here = bias.shape[0]
    channels = heads_here * HEAD_DIM
    group_size = HEADS * HEAD_DIM // NGROUPS
    tp_rank = lax.axis_index("tp")
    head_ids = tp_rank * heads_here + jnp.arange(heads_here, dtype=jnp.int32)
    head_groups = head_ids // (HEADS // NGROUPS)
    head_pick = (head_groups[:, None] == jnp.arange(NGROUPS, dtype=jnp.int32)[None, :]).astype(
        jnp.float32
    )
    chan_ids = tp_rank * channels + jnp.arange(channels, dtype=jnp.int32)
    chan_groups = chan_ids // group_size
    chan_pick = (chan_groups[:, None] == jnp.arange(NGROUPS, dtype=jnp.int32)[None, :]).astype(
        jnp.float32
    )

    def block_ordinal(resid):
        count = resid.shape[0]
        values = collect(resid, "tp", 1).astype(jnp.float32)
        scaled = (values * gain[None, :]).astype(jnp.bfloat16)
        proj = jnp.dot(scaled, w_inp, preferred_element_type=jnp.float32)
        step_raw = jnp.dot(scaled, w_step, preferred_element_type=jnp.float32)
        shared_raw = jnp.dot(scaled, w_shared, preferred_element_type=jnp.float32)
        squares = jnp.sum(values * values, axis=1, keepdims=True)
        proj, step_raw, shared_raw, squares = (proj, step_raw, shared_raw, squares)
        inv = lax.rsqrt(squares / HIDDEN_DIMENSION + 1e-05)
        pairs = (proj * inv).reshape(count, heads_here, 2, HEAD_DIM)
        xs = pairs[:, :, 0, :]
        gates = pairs[:, :, 1, :]
        step = jax.nn.softplus(step_raw * inv + bias[None, :])
        share = (shared_raw * inv).astype(jnp.bfloat16)
        gathered = collect(share, "tp", 1)
        grouped = gathered.astype(jnp.float32).reshape(count, 2 * STATE, NGROUPS)
        per_head = jnp.einsum("tng,hg->thn", grouped, head_pick, precision=lax.Precision.HIGHEST)
        bmat = per_head[:, :, :STATE]
        cmat = per_head[:, :, STATE:]
        rates = 0.0005 * jnp.exp2(code.astype(jnp.float32))
        cum = jnp.cumsum(-(step * rates[None, :]), axis=0)
        scores = jnp.einsum("thn,shn->tsh", cmat, bmat, precision=lax.Precision.HIGHEST)
        lower = jnp.arange(count)[:, None] >= jnp.arange(count)[None, :]
        decay = jnp.where(
            lower[:, :, None], jnp.exp(jnp.minimum(cum[:, None, :] - cum[None, :, :], 0.0)), 0.0
        )
        xdt = xs * step[:, :, None]
        intra = jnp.einsum("tsh,shp->thp", decay * scores, xdt, precision=lax.Precision.HIGHEST)
        total = cum[count - 1]
        tail = jnp.exp(total[None, :] - cum)
        local = jnp.einsum("shn,sh,shp->hnp", bmat, tail, xdt, precision=lax.Precision.HIGHEST)
        all_decay, all_states = (
            gather_at_once(total[None].astype(jnp.bfloat16), SEQ, 0).astype(jnp.float32),
            gather_at_once(local[None].astype(jnp.bfloat16), SEQ, 0).astype(jnp.float32),
        )
        mine = lax.axis_index(SEQ)
        inclusive = jnp.cumsum(all_decay, axis=0)
        exclusive = inclusive - all_decay
        upto = lax.dynamic_index_in_dim(exclusive, mine, 0, keepdims=True)
        order = jnp.arange(all_decay.shape[0])[:, None]
        weights = jnp.where(order < mine, jnp.exp(jnp.minimum(upto - inclusive, 0.0)), 0.0)
        entering = jnp.einsum("kh,khnp->hnp", weights, all_states, precision=lax.Precision.HIGHEST)
        inter = (
            jnp.einsum("thn,hnp->thp", cmat, entering, precision=lax.Precision.HIGHEST)
            * jnp.exp(cum)[:, :, None]
        )
        mixed = intra + inter + skip_coef[None, :, None] * xs
        gated = (mixed * jax.nn.silu(gates)).reshape(count, channels)
        group_part = jnp.dot(gated * gated, chan_pick, precision=lax.Precision.HIGHEST)
        group_total = taken_together(group_part, "tp")
        per_chan = jnp.dot(group_total, chan_pick.T, precision=lax.Precision.HIGHEST)
        gated = gated * lax.rsqrt(per_chan / group_size + 1e-05)
        normed = (gated * o_gain[None, :]).astype(jnp.bfloat16)
        summed = sum_at_owner(
            lax.dot_general(
                w_outp, normed, (((0,), (1,)), ((), ())), preferred_element_type=jnp.float32
            ).astype(jnp.bfloat16),
            "tp",
            0,
        )
        return (resid.astype(jnp.float32) + summed.T).astype(jnp.bfloat16)

    opening_round_produced = block_ordinal(waiting_batchlets[0])
    moved = shifted(opening_round_produced, "section", 1)
    start_here = lax.axis_index("section") == 0
    second_in = jnp.where(start_here, arriving_batchlet, moved)
    return block_ordinal(second_in)[None]


def solution(mesh):
    torus = Mesh(
        mesh.devices.reshape(mesh.shape["section"], 4, 2, mesh.shape["tp"]),
        ("section", "seq_0", "seq_1", "tp"),
    )
    return jax.shard_map(
        body,
        mesh=torus,
        in_specs=(
            P("section", SEQ, "tp"),
            P(SEQ, "tp"),
            P("section", None),
            P("section", None, "tp"),
            P("section", None, "tp"),
            P("section", "tp"),
            P("section", "tp"),
            P("section", None, "tp"),
            P("section", "tp"),
            P("section", "tp"),
            P("section", "tp", None),
        ),
        out_specs=P("section", SEQ, "tp"),
        check_vma=False,
    )
```

profile of v0, /device:TPU:24, one launch (start us, length us, event | category | flops | bytes accessed | tf_op | source)
XLA Modules:
  0.0 845.0 jit_solution(1672523044009423568)
XLA Ops:
  1.3 133.8 %all_to_all.40 = bf16[32,128,128]{1,2,0:T(8,128)(2,1)S(1)} all-to-all(bf16[32,128,128]{1,2,0:T(8,128)(2,1)S(1)} %broadcast_in_dim.56), channel_id=1, replica_groups=mesh['section'=4,'seq_0'=4,'seq_1'=2,'tp'=32] {'tp'}, dimensions={0} | all-to-all | bytes 2097152 | tf_op jit(solution)/shard_map/all_to_all | solution.py:17
  136.5 1.3 broadcast_in_dim.58
  137.7 7.5 all-to-all-start.1
  145.9 9.7 %all-gather.12 = bf16[4,1,4]{2,1,0:T(2,128)(2,1)S(1)} all-gather(bf16[1,1,4]{2,1,0:T(2,128)(2,1)S(1)} %convert_bitcast_fusion.3), channel_id=2, replica_groups=mesh['section'=4,'seq_0'=4,'seq_1'=2,'tp'=32] {'seq_0'}, dimensions={0}, use_global_device_ids=true | all-gather | bytes 40 | tf_op jit(solution)/shard_map/all_gather | solution.py:41
  155.7 1.8 all-gather.13
  157.5 3.0 fusion.18
  161.0 89.5 %all-to-all-done.1 = bf16[32,128,128]{1,2,0:T(8,128)(2,1)} async-done(((bf16[32,128,128]{1,2,0:T(8,128)(2,1)}), bf16[32,128,128]{1,2,0:T(8,128)(2,1)}, u32[]{:S(2)}, u32[]{:S(2)}) %all-to-all-start.1) | async-done | bytes 1048608 | tf_op jit(solution)/shard_map/all_to_all | solution.py:17
  250.4 2.2 copy.109
  255.0 1.9 all-gather.2
  256.9 12.7 %all-gather.4 = bf16[4,4,128,64]{2,3,1,0:T(8,128)(2,1)S(1)} all-gather(bf16[1,4,128,64]{2,3,1,0:T(8,128)(2,1)S(1)} %get-tuple-element.16), channel_id=6, replica_groups=mesh['section'=4,'seq_0'=4,'seq_1'=2,'tp'=32] {'seq_0'}, dimensions={0}, use_global_device_ids=true | all-gather | bytes 327680 | tf_op jit(solution)/shard_map/all_gather | solution.py:41
  269.6 2.2 all-gather.5
  271.8 12.8 %all-gather.3 = bf16[8,4,128,64]{2,3,1,0:T(8,128)(2,1)S(1)} all-gather(bf16[2,4,128,64]{2,3,1,0:T(8,128)(2,1)S(1)} %all-gather.2), channel_id=5, replica_groups=mesh['section'=4,'seq_0'=4,'seq_1'=2,'tp'=32] {'seq_0'}, dimensions={0}, use_global_device_ids=true | all-gather | bytes 655360 | tf_op jit(solution)/shard_map/all_gather | solution.py:41
  286.6 7.4 all-to-all-start.2
  294.1 29.8 %all-to-all-done.2 = f32[32,128,8]{1,2,0:T(8,128)S(1)} async-done(((f32[32,128,8]{1,2,0:T(8,128)}), f32[32,128,8]{1,2,0:T(8,128)S(1)}, u32[]{:S(2)}, u32[]{:S(2)}) %all-to-all-start.2) | async-done | bytes 131104 | tf_op jit(solution)/shard_map/all_to_all | solution.py:17
  325.1 106.8 %all_to_all.41 = bf16[32,128,128]{1,2,0:T(8,128)(2,1)S(1)} all-to-all(bf16[32,128,128]{1,2,0:T(8,128)(2,1)S(1)} %bitcast.242), channel_id=1, replica_groups=mesh['section'=4,'seq_0'=4,'seq_1'=2,'tp'=32] {'tp'}, dimensions={0} | all-to-all | bytes 2097152 | tf_op jit(solution)/shard_map/all_to_all | solution.py:71
  432.0 1.3 collective-permute-start
  433.3 4.5 collective-permute-done
  438.2 111.4 %all_to_all.42 = bf16[32,128,128]{1,2,0:T(8,128)(2,1)S(1)} all-to-all(bf16[32,128,128]{1,2,0:T(8,128)(2,1)S(1)} %broadcast_in_dim.64), channel_id=1, replica_groups=mesh['section'=4,'seq_0'=4,'seq_1'=2,'tp'=32] {'tp'}, dimensions={0} | all-to-all | bytes 2097152 | tf_op jit(solution)/shard_map/all_to_all | solution.py:17
  551.0 1.3 broadcast_in_dim.65
  552.3 7.5 all-to-all-start.5
  560.3 7.0 all-gather.14
  567.3 1.8 all-gather.15
  569.2 3.0 fusion.21
  572.6 91.8 %all-to-all-done.5 = bf16[32,128,128]{1,2,0:T(8,128)(2,1)} async-done(((bf16[32,128,128]{1,2,0:T(8,128)(2,1)}), bf16[32,128,128]{1,2,0:T(8,128)(2,1)}, u32[]{:S(2)}, u32[]{:S(2)}) %all-to-all-start.5) | async-done | bytes 1048608 | tf_op jit(solution)/shard_map/all_to_all | solution.py:17
  664.4 2.2 copy.129
  668.9 1.9 all-gather.8
  670.8 12.4 %all-gather.10 = bf16[4,4,128,64]{2,3,1,0:T(8,128)(2,1)S(1)} all-gather(bf16[1,4,128,64]{2,3,1,0:T(8,128)(2,1)S(1)} %get-tuple-element.14), channel_id=12, replica_groups=mesh['section'=4,'seq_0'=4,'seq_1'=2,'tp'=32] {'seq_0'}, dimensions={0}, use_global_device_ids=true | all-gather | bytes 327680 | tf_op jit(solution)/shard_map/all_gather | solution.py:41
  683.1 2.2 all-gather.11
  685.4 13.4 %all-gather.9 = bf16[8,4,128,64]{2,3,1,0:T(8,128)(2,1)S(1)} all-gather(bf16[2,4,128,64]{2,3,1,0:T(8,128)(2,1)S(1)} %all-gather.8), channel_id=11, replica_groups=mesh['section'=4,'seq_0'=4,'seq_1'=2,'tp'=32] {'seq_0'}, dimensions={0}, use_global_device_ids=true | all-gather | bytes 655360 | tf_op jit(solution)/shard_map/all_gather | solution.py:41
  700.8 7.6 all-to-all-start.6
  708.5 28.1 %all-to-all-done.6 = f32[32,128,8]{1,2,0:T(8,128)S(1)} async-done(((f32[32,128,8]{1,2,0:T(8,128)}), f32[32,128,8]{1,2,0:T(8,128)S(1)}, u32[]{:S(2)}, u32[]{:S(2)}) %all-to-all-start.6) | async-done | bytes 131104 | tf_op jit(solution)/shard_map/all_to_all | solution.py:17
  737.8 106.5 %all_to_all.43 = bf16[32,128,128]{1,2,0:T(8,128)(2,1)S(1)} all-to-all(bf16[32,128,128]{1,2,0:T(8,128)(2,1)S(1)} %bitcast.243), channel_id=1, replica_groups=mesh['section'=4,'seq_0'=4,'seq_1'=2,'tp'=32] {'tp'}, dimensions={0} | all-to-all | bytes 2097152 | tf_op jit(solution)/shard_map/all_to_all | solution.py:71
  (124 shorter events, 18.3 us)
Async XLA Ops:
  0.0 324.3 %copy-start = (bf16[1,256,4096]{2,1,0:T(8,128)(2,1)S(1)}, bf16[1,256,4096]{2,1,0:T(8,128)(2,1)}, u32[]{:S(2)}) copy-start(bf16[1,256,4096]{2,1,0:T(8,128)(2,1)} %param.21) | copy-start | bytes 6291460
  0.0 135.1 %copy-start.4 = (f32[1,4096]{1,0:T(1,128)S(1)}, f32[1,4096]{1,0:T(1,128)}, u32[]{:S(2)}) copy-start(f32[1,4096]{1,0:T(1,128)} %param.13) | copy-start | bytes 49156
  1.3 134.5 %copy-start.1 = (bf16[1,4096,128]{2,1,0:T(8,128)(2,1)S(1)}, bf16[1,4096,128]{2,1,0:T(8,128)(2,1)}, u32[]{:S(2)}) copy-start(bf16[1,4096,128]{2,1,0:T(8,128)(2,1)} %param.18) | copy-start | bytes 3145732
  136.3 9.0 %copy-start.13 = (s32[1,4]{1,0:T(1,128)S(1)}, s32[1,4]{1,0:T(1,128)}, u32[]{:S(2)}) copy-start(s32[1,4]{1,0:T(1,128)} %param.17) | copy-start | bytes 52
  136.3 9.0 %copy-start.9 = (bf16[1,4096,4]{1,2,0:T(4,128)(2,1)S(1)}, bf16[1,4096,4]{1,2,0:T(4,128)(2,1)}, u32[]{:S(2)}) copy-start(bf16[1,4096,4]{1,2,0:T(4,128)(2,1)} %param.15) | copy-start | bytes 98308
  136.3 9.0 %copy-start.14 = (f32[1,4]{1,0:T(1,128)S(1)}, f32[1,4]{1,0:T(1,128)}, u32[]{:S(2)}) copy-start(f32[1,4]{1,0:T(1,128)} %param.16) | copy-start | bytes 52
  137.7 112.7 %all-to-all-start.1 = ((bf16[32,128,128]{1,2,0:T(8,128)(2,1)}), bf16[32,128,128]{1,2,0:T(8,128)(2,1)}, u32[]{:S(2)}, u32[]{:S(2)}) async-start(bf16[32,128,128]{1,2,0:T(8,128)(2,1)} %broadcast_in_dim.58), calls=%async_computation.1 | async-start | bytes 2097152 | tf_op jit(solution)/shard_map/all_to_all | solution.py:17
  145.2 15.6 %copy-start.7 = (pred[8]{0:T(512)(128)(4,1)}, pred[8]{0:T(512)(128)(4,1)S(1)}, u32[]{:S(2)}) copy-start(pred[8]{0:T(512)(128)(4,1)S(1)} %iota_compare_fusion.7) | copy-start | bytes 28
  145.3 15.1 %copy-start.16 = (f32[4]{0:T(128)}, f32[4]{0:T(128)S(1)}, u32[]{:S(2)}) copy-start(f32[4]{0:T(128)S(1)} %multiply_bitcast_fusion) | copy-start | bytes 52
  256.9 28.1 %copy-start.6 = (f32[1,4]{1,0:T(1,128)S(1)}, f32[1,4]{1,0:T(1,128)}, u32[]{:S(2)}) copy-start(f32[1,4]{1,0:T(1,128)} %param.19) | copy-start | bytes 52
  271.8 52.2 %copy-start.11 = (f32[1,256]{1,0:T(1,128)S(1)}, f32[1,256]{1,0:T(1,128)}, u32[]{:S(2)}) copy-start(f32[1,256]{1,0:T(1,128)} %param.20) | copy-start | bytes 3076
  286.6 37.3 %all-to-all-start.2 = ((f32[32,128,8]{1,2,0:T(8,128)}), f32[32,128,8]{1,2,0:T(8,128)S(1)}, u32[]{:S(2)}, u32[]{:S(2)}) async-start(f32[32,128,8]{1,2,0:T(8,128)} %broadcast_in_dim.63), calls=%async_computation.2 | async-start | bytes 262144 | tf_op jit(solution)/shard_map/all_to_all | solution.py:17
  325.1 106.9 %copy-start.3 = (bf16[1,128,128]{2,1,0:T(8,128)(2,1)S(1)}, bf16[1,128,128]{2,1,0:T(8,128)(2,1)}, u32[]{:S(2)}) copy-start(bf16[1,128,128]{2,1,0:T(8,128)(2,1)} %param.11) | copy-start | bytes 98308
  325.1 112.8 %copy-start.5 = (bf16[128,128]{1,0:T(8,128)(2,1)S(1)}, bf16[128,128]{1,0:T(8,128)(2,1)}, u32[]{:S(2)}) copy-start(bf16[128,128]{1,0:T(8,128)(2,1)} %param.12) | copy-start | bytes 98308
  432.0 5.8 collective-permute-start
  438.2 112.1 %copy-start.2 = (bf16[1,4096,128]{2,1,0:T(8,128)(2,1)S(1)}, bf16[1,4096,128]{2,1,0:T(8,128)(2,1)}, u32[]{:S(2)}) copy-start(bf16[1,4096,128]{2,1,0:T(8,128)(2,1)} %param.18) | copy-start | bytes 3145732
  550.8 8.9 %copy-start.10 = (bf16[1,4096,4]{1,2,0:T(4,128)(2,1)S(1)}, bf16[1,4096,4]{1,2,0:T(4,128)(2,1)}, u32[]{:S(2)}) copy-start(bf16[1,4096,4]{1,2,0:T(4,128)(2,1)} %param.15) | copy-start | bytes 98308
  550.8 8.9 %copy-start.15 = (f32[1,4]{1,0:T(1,128)S(1)}, f32[1,4]{1,0:T(1,128)}, u32[]{:S(2)}) copy-start(f32[1,4]{1,0:T(1,128)} %param.16) | copy-start | bytes 52
  550.9 8.9 %copy-start.17 = (f32[4]{0:T(128)S(1)}, f32[4]{0:T(128)}, u32[]{:S(2)}) copy-start(f32[4]{0:T(128)} %copy-done.16) | copy-start | bytes 52
  552.3 112.1 %all-to-all-start.5 = ((bf16[32,128,128]{1,2,0:T(8,128)(2,1)}), bf16[32,128,128]{1,2,0:T(8,128)(2,1)}, u32[]{:S(2)}, u32[]{:S(2)}) async-start(bf16[32,128,128]{1,2,0:T(8,128)(2,1)} %broadcast_in_dim.65), calls=%async_computation.5 | async-start | bytes 2097152 | tf_op jit(solution)/shard_map/all_to_all | solution.py:17
  569.2 3.4 copy-start.8
  685.3 51.4 %copy-start.12 = (f32[1,256]{1,0:T(1,128)S(1)}, f32[1,256]{1,0:T(1,128)}, u32[]{:S(2)}) copy-start(f32[1,256]{1,0:T(1,128)} %param.20) | copy-start | bytes 3076
  700.8 35.9 %all-to-all-start.6 = ((f32[32,128,8]{1,2,0:T(8,128)}), f32[32,128,8]{1,2,0:T(8,128)S(1)}, u32[]{:S(2)}, u32[]{:S(2)}) async-start(f32[32,128,8]{1,2,0:T(8,128)} %broadcast_in_dim.69), calls=%async_computation.6 | async-start | bytes 262144 | tf_op jit(solution)/shard_map/all_to_all | solution.py:17
where the time goes:
time: 846 us; the launch traced here: 845 us
  blocking collectives  538 us (64%)
  waiting for transfers between devices  244 us (29%)
  starting transfers between devices  31.3 us (4%)
  matrix products  15.1 us (2%)
  local copies, waits for them, and re-layouts  12.4 us (1%)
    all_to_all x2, blocking collectives, copy_for_each(): lax.all_to_all(jnp.broadcast_to(value[None], (peers, *value.shape)), axis...  245 us
    all_to_all x4, waiting for transfers between devices, copy_for_each(): lax.all_to_all(jnp.broadcast_to(value[None], (peers, *value.shape)), axis...  239 us
    all_to_all x2, blocking collectives, sum_at_owner(): parts = lax.all_to_all(split_up(value, dim, peers), axis, 0, 0, tiled=True)  213 us
    all_gather x12, blocking collectives, stacked_from(): parts = lax.all_gather(parts, axes[k], axis=0, tiled=True)  79.7 us
    all_to_all x4, starting transfers between devices, copy_for_each(): lax.all_to_all(jnp.broadcast_to(value[None], (peers, *value.shape)), axis...  30 us
  transfers between devices with their start and end apart: 5, of which 5 were waited for; matrix products, arithmetic and copies ran while one was open for 1% of the time, Pallas kernels for 0%

commit v1 on v0

v1 whole, which is shorter than its diff:
```python
import jax
import jax.numpy as jnp
from jax import lax
from jax.sharding import Mesh
from jax.sharding import PartitionSpec as P

HEAD_DIM = 64
SEQ = ("seq_0", "seq_1")
TP = ("tp_hi", "tp_lo")
BF = jnp.bfloat16
F32 = jnp.float32


def swap(value, axis):
    return lax.all_to_all(value, axis, 0, 0, tiled=True)


def spread(value, axis):
    return swap(jnp.broadcast_to(value[None], (lax.axis_size(axis), *value.shape)), axis)


def in_two(value):
    high = value.astype(BF)
    return high, (value - high.astype(F32)).astype(BF)


def dot(a, b, dims=((1,), (0,))):
    return lax.dot_general(a, b, (dims, ((), ())), preferred_element_type=F32)


def body(
    waiting_batchlets,
    arriving_batchlet,
    entry_rescale_factor,
    entry_projection_matrix,
    timescale_projection,
    timescale_offset,
    channel_forgetting_rate,
    state_read_write_matrix,
    direct_passthrough,
    closing_rescale_factor,
    closing_projection_matrix,
):
    gain = entry_rescale_factor[0]
    w_inp = entry_projection_matrix[0]
    w_step = timescale_projection[0]
    bias = timescale_offset[0]
    rates = 0.0005 * jnp.exp2(channel_forgetting_rate[0].astype(F32))
    w_shared = state_read_write_matrix[0]
    skip_coef = direct_passthrough[0]
    o_gain = closing_rescale_factor[0]
    w_outp = closing_projection_matrix[0]

    hi = lax.axis_size("tp_hi")
    lo = lax.axis_size("tp_lo")
    pieces = lax.axis_size(SEQ)
    chips = lax.axis_size("seq_0")
    chip = lax.axis_index("seq_0")
    core = lax.axis_index("seq_1")
    hidden = w_inp.shape[0]
    heads = bias.shape[0]
    channels = heads * HEAD_DIM
    group_size = channels * lo
    here = w_shared.shape[1]
    per = here // hi

    rows = hidden // pieces
    strip = lax.dynamic_slice_in_dim(w_shared, lax.axis_index(SEQ) * rows, rows, 0)
    strip = strip.T.reshape(per, hi, rows).transpose(1, 0, 2)
    own = swap(strip, "tp_hi").reshape(here, rows)
    w_bc = spread(own, SEQ).transpose(1, 0, 2).reshape(here, hidden)

    def mixer(resid):
        count = resid.shape[0]
        far = spread(resid, "tp_hi")
        near = spread(far, "tp_lo")
        values = near.transpose(2, 1, 0, 3).reshape(count, hidden).astype(F32)
        scaled = (values * gain[None, :]).astype(BF)
        inv = lax.rsqrt(jnp.sum(values * values, axis=1, keepdims=True) / hidden + 1e-05)
        share = (dot(scaled, w_bc, ((1,), (1,))) * inv).astype(BF)
        step = jax.nn.softplus(dot(scaled, w_step) * inv + bias[None, :])
        pairs = (dot(scaled, w_inp) * inv).reshape(count, heads, 2, HEAD_DIM)
        xs = pairs[:, :, 0, :]
        gates = pairs[:, :, 1, :]

        cum = jnp.cumsum(-(step * rates[None, :]), axis=0)
        total = cum[count - 1]
        totals = spread(jnp.broadcast_to(total[:, None], (heads, 128)), SEQ)[:, :, 0]

        shared = spread(share, "tp_lo")
        half = here // 2
        bmat = shared[:, :, :half].transpose(1, 0, 2).reshape(count, lo * half)
        cmat = shared[:, :, half:].transpose(1, 0, 2).reshape(count, lo * half)

        xdt = xs * step[:, :, None]
        tail = jnp.exp(total[None, :] - cum)
        pushed = (xdt * tail[:, :, None]).reshape(count, channels).astype(BF)
        local = dot(bmat, pushed, ((0,), (0,)))
        states = spread(local.astype(BF), "seq_0").astype(F32)

        edges = jnp.cumsum(totals, axis=0)
        first = lax.dynamic_index_in_dim(edges - totals, 2 * chip, 0, keepdims=True)
        reach = jnp.where(
            jnp.arange(pieces)[:, None] < 2 * chip, jnp.exp(jnp.minimum(first - edges, 0.0)), 0.0
        )
        mine = lax.dynamic_index_in_dim(reach.reshape(chips, 2, heads), core, 1, keepdims=False)
        mine = jnp.repeat(mine, HEAD_DIM, axis=1)
        before = jnp.sum(states * mine[:, None, :], axis=0)
        across = jnp.exp(lax.dynamic_index_in_dim(totals, 2 * chip, 0, keepdims=True))
        across = jnp.repeat(across, HEAD_DIM, axis=1)
        sent = jnp.where(core == 0, before * across + local, before)
        other = lax.ppermute(sent.astype(BF), "seq_1", [(0, 1), (1, 0)]).astype(F32)
        entering = jnp.where(core == 0, before, before * across) + other

        scores = dot(cmat, bmat, ((1,), (1,)))
        lower = jnp.arange(count)[:, None] >= jnp.arange(count)[None, :]
        decay = jnp.where(
            lower[None], jnp.exp(jnp.minimum(cum.T[:, :, None] - cum.T[:, None, :], 0.0)), 0.0
        )
        intra = jnp.einsum(
            "hts,shp->thp",
            (decay * scores[None]).astype(BF),
            xdt.astype(BF),
            preferred_element_type=F32,
        )
        inter = dot(cmat, entering.astype(BF)).reshape(count, heads, HEAD_DIM)
        inter = inter * jnp.exp(cum)[:, :, None]
        mixed = intra + inter + skip_coef[None, :, None] * xs
        gated = (mixed * jax.nn.silu(gates)).reshape(count, channels)
        part = jnp.sum(gated * gated, axis=1)
        normed = (gated * o_gain[None, :]).astype(BF)
        shares = dot(normed, w_outp).astype(BF)
        shares = shares.reshape(count, hi, lo, -1).transpose(2, 1, 0, 3)
        width = shares.shape[-1]
        shares = shares.reshape(lo, hi * count, width)
        notes = jnp.pad(jnp.stack(in_two(part)), ((0, 14), (0, 0)))
        notes = jnp.broadcast_to(notes[None], (lo, *notes.shape))
        got = swap(jnp.concatenate([shares, notes], axis=1), "tp_lo")
        square = jnp.sum(got[:, hi * count : hi * count + 2].astype(F32), axis=(0, 1))
        unit = lax.rsqrt(square / group_size + 1e-05)
        summed = jnp.sum(got[:, : hi * count].astype(F32), axis=0).reshape(hi, count, width)
        summed = (summed * unit[None, :, None]).astype(BF)
        summed = jnp.sum(swap(summed, "tp_hi").astype(F32), axis=0)
        return (resid.astype(F32) + summed).astype(BF)

    opening = mixer(waiting_batchlets[0])
    sections = lax.axis_size("section")
    moved = lax.ppermute(opening, "section", [(i, i + 1) for i in range(sections - 1)])
    second_in = jnp.where(lax.axis_index("section") == 0, arriving_batchlet, moved)
    return mixer(second_in)[None]


def solution(mesh, cut=None):
    sections, seq, tp = (mesh.shape[name] for name in ("section", "seq", "tp"))
    near = cut or 4
    torus = Mesh(
        mesh.devices.reshape(sections, seq // 2, 2, tp // near, near),
        ("section", *SEQ, *TP),
    )
    return jax.shard_map(
        body,
        mesh=torus,
        in_specs=(
            P("section", SEQ, TP),
            P(SEQ, TP),
            P("section", None),
            P("section", None, TP),
            P("section", None, TP),
            P("section", TP),
            P("section", TP),
            P("section", None, TP),
            P("section", TP),
            P("section", TP),
            P("section", TP, None),
        ),
        out_specs=P("section", SEQ, TP),
        check_vma=False,
    )
```

time: 846 us -> 485 us (0.57)
  blocking collectives: 538 us -> 250 us
  waiting for transfers between devices: 244 us -> 92.5 us
  starting transfers between devices: 31.3 us -> 69.6 us
  local copies, waits for them, and re-layouts: 12.4 us -> 31.8 us
  other arithmetic: 3.74 us -> 13 us
    all_to_all x4 -> x7, blocking collectives: 458 us -> 250 us  [swap(): return lax.all_to_all(value, axis, 0, 0, tiled=True)]
    all_to_all x4 -> x9, waiting for transfers between devices: 239 us -> 87.8 us  [swap(): return lax.all_to_all(value, axis, 0, 0, tiled=True)]
    all_gather x12 -> x0, blocking collectives: 79.7 us -> none  [stacked_from(): parts = lax.all_gather(parts, axes[k], axis=0, tiled=True)]
    all_to_all x4 -> x9, starting transfers between devices: 30 us -> 64.5 us  [swap(): return lax.all_to_all(value, axis, 0, 0, tiled=True)]
    dot_general x22 -> x16, matrix products: 15.1 us -> 19 us  [the longest x14 16.3 us: dot(): return lax.dot_general(a, b, (dims, ((), ())), preferred_element_type=F32)]
  transfers between devices with their start and end apart: 5 -> 12, of which waited for: 5 -> 10; matrix products, arithmetic and copies ran while one was open for 1% -> 6% of each run, Pallas kernels for 0% -> 0%
where the time goes in v1:
time: 485 us; the launch traced here: 476 us
  blocking collectives  250 us (52%)
  waiting for transfers between devices  92.5 us (19%)
  starting transfers between devices  69.6 us (14%)
  local copies, waits for them, and re-layouts  31.8 us (7%)
  matrix products  19 us (4%)
  other arithmetic  13 us (3%)
    all_to_all x7, blocking collectives, swap(): return lax.all_to_all(value, axis, 0, 0, tiled=True)  250 us
    all_to_all x9, waiting for transfers between devices, swap(): return lax.all_to_all(value, axis, 0, 0, tiled=True)  87.8 us
    all_to_all x9, starting transfers between devices, swap(): return lax.all_to_all(value, axis, 0, 0, tiled=True)  64.5 us
    dot_general x14, matrix products, dot(): return lax.dot_general(a, b, (dims, ((), ())), preferred_element_type=F32)  16.3 us
  transfers between devices with their start and end apart: 12, of which 10 were waited for; matrix products, arithmetic and copies ran while one was open for 6% of the time, Pallas kernels for 0%

profile of v1, /device:TPU:24, one launch (start us, length us, event | category | flops | bytes accessed | tf_op | source)
XLA Modules:
  0.0 476.5 jit_solution(8018182096116245027)
XLA Ops:
  1.9 28.3 %all-to-all-start.2 = ((bf16[8,16,512]{2,1,0:T(8,128)(2,1)}), bf16[8,16,512]{2,1,0:T(8,128)(2,1)S(1)}, u32[]{:S(2)}, u32[]{:S(2)}) async-start(bf16[8,16,512]{2,1,0:T(8,128)(2,1)} %copy.142), calls=%async_computation.2 | async-start | bytes 262144 | tf_op jit(solution)/shard_map/all_to_all | solution.py:15
  31.1 26.9 %all-to-all-done.2 = bf16[8,16,512]{2,1,0:T(8,128)(2,1)S(1)} async-done(((bf16[8,16,512]{2,1,0:T(8,128)(2,1)}), bf16[8,16,512]{2,1,0:T(8,128)(2,1)S(1)}, u32[]{:S(2)}, u32[]{:S(2)}) %all-to-all-start.2) | async-done | bytes 131104 | tf_op jit(solution)/shard_map/all_to_all | solution.py:15
  58.0 36.7 %all_to_all.80 = bf16[8,128,128]{1,2,0:T(8,128)(2,1)S(1)} all-to-all(bf16[8,128,128]{1,2,0:T(8,128)(2,1)S(1)} %broadcast_in_dim.68), channel_id=1, replica_groups=mesh['section'=4,'seq_0'=4,'seq_1'=2,'tp_hi'=8,'tp_lo'=4] {'tp_hi'}, dimensions={0} | all-to-all | bytes 524288 | tf_op jit(solution)/shard_map/all_to_all | solution.py:15
  96.0 10.8 %all-to-all-start.1 = ((bf16[4,8,128,128]{2,3,1,0:T(8,128)(2,1)}), bf16[4,8,128,128]{2,3,1,0:T(8,128)(2,1)S(1)}, u32[]{:S(2)}, u32[]{:S(2)}) async-start(bf16[4,8,128,128]{2,3,1,0:T(8,128)(2,1)} %broadcast_in_dim.69), calls=%async_computation.1 | async-start | bytes 2097152 | tf_op jit(solution)/shard_map/all_to_all | solution.py:15
  107.5 24.4 %all-to-all-done.1 = bf16[4,8,128,128]{2,3,1,0:T(8,128)(2,1)S(1)} async-done(((bf16[4,8,128,128]{2,3,1,0:T(8,128)(2,1)}), bf16[4,8,128,128]{2,3,1,0:T(8,128)(2,1)S(1)}, u32[]{:S(2)}, u32[]{:S(2)}) %all-to-all-start.1) | async-done | bytes 1048608 | tf_op jit(solution)/shard_map/all_to_all | solution.py:15
  133.3 4.3 all-to-all-start.3
  137.6 1.8 fusion.9
  141.5 12.0 %all-to-all-done.3 = bf16[8,128,512]{1,2,0:T(8,128)(2,1)S(1)} async-done(((bf16[8,128,512]{1,2,0:T(8,128)(2,1)}), bf16[8,128,512]{1,2,0:T(8,128)(2,1)S(1)}, u32[]{:S(2)}, u32[]{:S(2)}) %all-to-all-start.3) | async-done | bytes 1048608 | tf_op jit(solution)/shard_map/all_to_all | solution.py:15
  154.2 3.3 all-to-all-start.6
  157.5 1.7 fusion.22
  159.3 3.5 all-to-all-done.6
  163.5 3.3 all-to-all-start.4
  168.1 3.2 fusion.10
  175.9 4.1 all-to-all-start.5
  181.3 8.5 %all-to-all-done.5 = bf16[4,256,256]{2,1,0:T(8,128)(2,1)} async-done(((bf16[4,256,256]{2,1,0:T(8,128)(2,1)}), bf16[4,256,256]{2,1,0:T(8,128)(2,1)}, u32[]{:S(2)}, u32[]{:S(2)}) %all-to-all-start.5) | async-done | bytes 524320 | tf_op jit(solution)/shard_map/all_to_all | solution.py:15
  192.6 1.9 collective-permute-start
  195.1 1.9 reduce.15
  207.1 2.6 reshape.340
  211.4 31.3 %all_to_all.81 = bf16[4,1040,128]{2,1,0:T(8,128)(2,1)S(1)} all-to-all(bf16[4,1040,128]{2,1,0:T(8,128)(2,1)S(1)} %pad_maximum_fusion), channel_id=1, replica_groups=mesh['section'=4,'seq_0'=4,'seq_1'=2,'tp_hi'=8,'tp_lo'=4] {'tp_lo'}, dimensions={0} | all-to-all | bytes 2129920 | tf_op jit(solution)/shard_map/all_to_all | solution.py:15
  243.0 36.8 %all_to_all.82 = bf16[8,128,128]{2,1,0:T(8,128)(2,1)S(1)} all-to-all(bf16[8,128,128]{2,1,0:T(8,128)(2,1)S(1)} %multiply_convert_fusion.1), channel_id=1, replica_groups=mesh['section'=4,'seq_0'=4,'seq_1'=2,'tp_hi'=8,'tp_lo'=4] {'tp_hi'}, dimensions={0} | all-to-all | bytes 524288 | tf_op jit(solution)/shard_map/all_to_all | solution.py:15
  281.2 4.5 collective-permute-done.1
  285.9 51.6 %all_to_all.83 = bf16[8,128,128]{1,2,0:T(8,128)(2,1)S(1)} all-to-all(bf16[8,128,128]{1,2,0:T(8,128)(2,1)S(1)} %broadcast_in_dim.80), channel_id=1, replica_groups=mesh['section'=4,'seq_0'=4,'seq_1'=2,'tp_hi'=8,'tp_lo'=4] {'tp_hi'}, dimensions={0} | all-to-all | bytes 524288 | tf_op jit(solution)/shard_map/all_to_all | solution.py:15
  337.7 19.9 %all_to_all.84 = bf16[4,8,128,128]{2,3,1,0:T(8,128)(2,1)S(1)} all-to-all(bf16[4,8,128,128]{2,3,1,0:T(8,128)(2,1)S(1)} %broadcast_in_dim.81), channel_id=1, replica_groups=mesh['section'=4,'seq_0'=4,'seq_1'=2,'tp_hi'=8,'tp_lo'=4] {'tp_lo'}, dimensions={0} | all-to-all | bytes 2097152 | tf_op jit(solution)/shard_map/all_to_all | solution.py:15
  360.6 3.3 all-to-all-start.13
  365.8 3.5 all-to-all-done.13
  369.9 3.3 all-to-all-start.11
  373.9 3.3 fusion.13
  381.0 3.6 all-to-all-start.12
  385.3 7.6 %all-to-all-done.12 = bf16[4,256,256]{2,1,0:T(8,128)(2,1)S(1)} async-done(((bf16[4,256,256]{2,1,0:T(8,128)(2,1)}), bf16[4,256,256]{2,1,0:T(8,128)(2,1)S(1)}, u32[]{:S(2)}, u32[]{:S(2)}) %all-to-all-start.12) | async-done | bytes 524320 | tf_op jit(solution)/shard_map/all_to_all | solution.py:15
  393.1 1.9 collective-permute-start.2
  401.8 31.0 %all_to_all.85 = bf16[4,1040,128]{2,1,0:T(8,128)(2,1)S(1)} all-to-all(bf16[4,1040,128]{2,1,0:T(8,128)(2,1)S(1)} %pad_maximum_fusion.1), channel_id=1, replica_groups=mesh['section'=4,'seq_0'=4,'seq_1'=2,'tp_hi'=8,'tp_lo'=4] {'tp_lo'}, dimensions={0} | all-to-all | bytes 2129920 | tf_op jit(solution)/shard_map/all_to_all | solution.py:15
  433.2 42.7 %all_to_all.86 = bf16[8,128,128]{2,1,0:T(8,128)(2,1)S(1)} all-to-all(bf16[8,128,128]{2,1,0:T(8,128)(2,1)S(1)} %multiply_convert_fusion), channel_id=1, replica_groups=mesh['section'=4,'seq_0'=4,'seq_1'=2,'tp_hi'=8,'tp_lo'=4] {'tp_hi'}, dimensions={0} | all-to-all | bytes 524288 | tf_op jit(solution)/shard_map/all_to_all | solution.py:15
  (166 shorter events, 52.4 us)
Async XLA Ops:
  0.0 205.6 %copy-start = (bf16[1,256,4096]{2,1,0:T(8,128)(2,1)S(1)}, bf16[1,256,4096]{2,1,0:T(8,128)(2,1)}, u32[]{:S(2)}) copy-start(bf16[1,256,4096]{2,1,0:T(8,128)(2,1)} %param.21) | copy-start | bytes 6291460
  1.9 56.1 %all-to-all-start.2 = ((bf16[8,16,512]{2,1,0:T(8,128)(2,1)}), bf16[8,16,512]{2,1,0:T(8,128)(2,1)S(1)}, u32[]{:S(2)}, u32[]{:S(2)}) async-start(bf16[8,16,512]{2,1,0:T(8,128)(2,1)} %copy.142), calls=%async_computation.2 | async-start | bytes 262144 | tf_op jit(solution)/shard_map/all_to_all | solution.py:15
  31.1 76.3 %copy-start.17 = (s32[1,4]{1,0:T(1,128)S(1)}, s32[1,4]{1,0:T(1,128)}, u32[]{:S(2)}) copy-start(s32[1,4]{1,0:T(1,128)} %param.17) | copy-start | bytes 52
  96.0 35.9 %all-to-all-start.1 = ((bf16[4,8,128,128]{2,3,1,0:T(8,128)(2,1)}), bf16[4,8,128,128]{2,3,1,0:T(8,128)(2,1)S(1)}, u32[]{:S(2)}, u32[]{:S(2)}) async-start(bf16[4,8,128,128]{2,3,1,0:T(8,128)(2,1)} %broadcast_in_dim.69), calls=%async_computation.1 | async-start | bytes 2097152 | tf_op jit(solution)/shard_map/all_to_all | solution.py:15
  106.8 30.8 %copy-start.8 = (f32[1,4096]{1,0:T(1,128)S(1)}, f32[1,4096]{1,0:T(1,128)}, u32[]{:S(2)}) copy-start(f32[1,4096]{1,0:T(1,128)} %param.13) | copy-start | bytes 49156
  107.4 32.0 %copy-start.20 = (f32[4]{0:T(128)}, f32[4]{0:T(128)S(1)}, u32[]{:S(2)}) copy-start(f32[4]{0:T(128)S(1)} %multiply_bitcast_fusion) | copy-start | bytes 52
  131.9 1.3 copy-start.3
  133.2 7.2 %copy-start.15 = (bf16[1,4096,4]{1,2,0:T(4,128)(2,1)S(1)}, bf16[1,4096,4]{1,2,0:T(4,128)(2,1)}, u32[]{:S(2)}) copy-start(bf16[1,4096,4]{1,2,0:T(4,128)(2,1)} %param.15) | copy-start | bytes 98308
  133.2 7.2 %copy-start.18 = (f32[1,4]{1,0:T(1,128)S(1)}, f32[1,4]{1,0:T(1,128)}, u32[]{:S(2)}) copy-start(f32[1,4]{1,0:T(1,128)} %param.16) | copy-start | bytes 52
  133.3 20.2 %all-to-all-start.3 = ((bf16[8,128,512]{1,2,0:T(8,128)(2,1)}), bf16[8,128,512]{1,2,0:T(8,128)(2,1)S(1)}, u32[]{:S(2)}, u32[]{:S(2)}) async-start(bf16[8,128,512]{1,2,0:T(8,128)(2,1)} %broadcast_in_dim.72), calls=%async_computation.3 | async-start | bytes 2097152 | tf_op jit(solution)/shard_map/all_to_all | solution.py:15
  139.4 28.0 %copy-start.12 = (f32[128]{0:T(128)}, f32[128]{0:T(128)S(1)}, u32[]{:S(2)}) copy-start(f32[128]{0:T(128)S(1)} %add_rsqrt_fusion.3) | copy-start | bytes 1540
  141.5 25.9 %copy-start.4 = (f32[128,4]{1,0:T(8,128)}, f32[128,4]{1,0:T(8,128)S(1)}, u32[]{:S(2)}) copy-start(f32[128,4]{1,0:T(8,128)S(1)} %reduce_window_sum.38) | copy-start | bytes 6148
  154.2 8.6 %all-to-all-start.6 = ((f32[8,4,128]{2,1,0:T(4,128)}), f32[8,4,128]{2,1,0:T(4,128)S(1)}, u32[]{:S(2)}, u32[]{:S(2)}) async-start(f32[8,4,128]{2,1,0:T(4,128)} %broadcast_in_dim_broadcast_in_dim_broadcast_in_dim.4), calls=%async_computation.6 | async-start | bytes 32768 | tf_op jit(solution)/shard_map/all_to_all | solution.py:15
  163.5 10.0 %all-to-all-start.4 = ((bf16[4,128,128]{1,2,0:T(8,128)(2,1)}), bf16[4,128,128]{1,2,0:T(8,128)(2,1)S(1)}, u32[]{:S(2)}, u32[]{:S(2)}) async-start(bf16[4,128,128]{1,2,0:T(8,128)(2,1)} %broadcast_in_dim.73), calls=%async_computation.4 | async-start | bytes 262144 | tf_op jit(solution)/shard_map/all_to_all | solution.py:15
  172.2 8.0 %copy-start.13 = (pred[4,1]{1,0:T(4,128)(4,1)S(1)}, pred[4,1]{1,0:T(4,128)(4,1)}, u32[]{:S(2)}) copy-start(pred[4,1]{1,0:T(4,128)(4,1)} %constant_dynamic-slice_fusion) | copy-start | bytes 16
  175.9 13.9 %all-to-all-start.5 = ((bf16[4,256,256]{2,1,0:T(8,128)(2,1)}), bf16[4,256,256]{2,1,0:T(8,128)(2,1)}, u32[]{:S(2)}, u32[]{:S(2)}) async-start(bf16[4,256,256]{2,1,0:T(8,128)(2,1)} %broadcast_in_dim.74), calls=%async_computation.5 | async-start | bytes 1048576 | tf_op jit(solution)/shard_map/all_to_all | solution.py:15
  181.3 11.3 %copy-start.11 = (f32[256]{0:T(256)}, f32[256]{0:T(256)S(1)}, u32[]{:S(2)}) copy-start(f32[256]{0:T(256)S(1)} %broadcast_in_dim.78) | copy-start | bytes 3076
  192.6 9.5 %collective-permute-start = (bf16[256,256]{1,0:T(8,128)(2,1)}, bf16[256,256]{1,0:T(8,128)(2,1)}, u32[]{:S(2)}, u32[]{:S(2)}) collective-permute-start(bf16[256,256]{1,0:T(8,128)(2,1)} %fusion.28), channel_id=1, source_target_pairs={{0,32},{32,0},{1,33},{33,1},{2,34},{34,2},{3,35},{35,3},{4,36},{36... | collective-permute-start | bytes 393224 | tf_op jit(solution)/shard_map/ppermute | solution.py:112
  242.7 37.1 %copy-start.7 = (bf16[1,128,128]{2,1,0:T(8,128)(2,1)S(1)}, bf16[1,128,128]{2,1,0:T(8,128)(2,1)}, u32[]{:S(2)}) copy-start(bf16[1,128,128]{2,1,0:T(8,128)(2,1)} %param.11) | copy-start | bytes 98308
  242.7 43.0 %copy-start.10 = (bf16[128,128]{1,0:T(8,128)(2,1)S(1)}, bf16[128,128]{1,0:T(8,128)(2,1)}, u32[]{:S(2)}) copy-start(bf16[128,128]{1,0:T(8,128)(2,1)} %param.12) | copy-start | bytes 98308
  279.9 5.8 %collective-permute-start.1 = (bf16[128,128]{1,0:T(8,128)(2,1)S(1)}, bf16[128,128]{1,0:T(8,128)(2,1)S(1)}, u32[]{:S(2)}, u32[]{:S(2)}) collective-permute-start(bf16[128,128]{1,0:T(8,128)(2,1)S(1)} %add_convert_fusion.1), channel_id=1, source_target_pairs={{0,256},{256,512},{512,768},{1,257},{257,513},{513,769},{2,258},{2... | collective-permute-start | bytes 98312 | tf_op jit(solution)/shard_map/ppermute | solution.py:148
  285.8 71.8 %copy-start.9 = (f32[1,4096]{1,0:T(1,128)S(1)}, f32[1,4096]{1,0:T(1,128)}, u32[]{:S(2)}) copy-start(f32[1,4096]{1,0:T(1,128)} %param.13) | copy-start | bytes 49156
  337.7 21.7 %copy-start.16 = (bf16[1,4096,4]{1,2,0:T(4,128)(2,1)S(1)}, bf16[1,4096,4]{1,2,0:T(4,128)(2,1)}, u32[]{:S(2)}) copy-start(bf16[1,4096,4]{1,2,0:T(4,128)(2,1)} %param.15) | copy-start | bytes 98308
  337.7 21.7 %copy-start.19 = (f32[1,4]{1,0:T(1,128)S(1)}, f32[1,4]{1,0:T(1,128)}, u32[]{:S(2)}) copy-start(f32[1,4]{1,0:T(1,128)} %param.16) | copy-start | bytes 52
  337.7 21.6 %copy-start.21 = (f32[4]{0:T(128)S(1)}, f32[4]{0:T(128)}, u32[]{:S(2)}) copy-start(f32[4]{0:T(128)} %copy-done.20) | copy-start | bytes 52
  360.6 8.6 %all-to-all-start.13 = ((f32[8,4,128]{2,1,0:T(4,128)}), f32[8,4,128]{2,1,0:T(4,128)S(1)}, u32[]{:S(2)}, u32[]{:S(2)}) async-start(f32[8,4,128]{2,1,0:T(4,128)} %broadcast_in_dim_broadcast_in_dim_broadcast_in_dim.5), calls=%async_computation.13 | async-start | bytes 32768 | tf_op jit(solution)/shard_map/all_to_all | solution.py:15
  369.9 9.4 %all-to-all-start.11 = ((bf16[4,128,128]{1,2,0:T(8,128)(2,1)}), bf16[4,128,128]{1,2,0:T(8,128)(2,1)S(1)}, u32[]{:S(2)}, u32[]{:S(2)}) async-start(bf16[4,128,128]{1,2,0:T(8,128)(2,1)} %broadcast_in_dim.82), calls=%async_computation.11 | async-start | bytes 262144 | tf_op jit(solution)/shard_map/all_to_all | solution.py:15
  377.4 2.6 copy-start.5
  377.4 7.5 %copy-start.14 = (pred[4,1]{1,0:T(4,128)(4,1)S(1)}, pred[4,1]{1,0:T(4,128)(4,1)}, u32[]{:S(2)}) copy-start(pred[4,1]{1,0:T(4,128)(4,1)} %constant_dynamic-slice_fusion) | copy-start | bytes 16
  381.0 15.5 %copy-start.6 = (bf16[4,128,64]{1,2,0:T(8,128)(2,1)S(1)}, bf16[4,128,64]{1,2,0:T(8,128)(2,1)}, u32[]{:S(2)}) copy-start(bf16[4,128,64]{1,2,0:T(8,128)(2,1)} %get-tuple-element.12) | copy-start | bytes 196612
  381.0 11.9 %all-to-all-start.12 = ((bf16[4,256,256]{2,1,0:T(8,128)(2,1)}), bf16[4,256,256]{2,1,0:T(8,128)(2,1)S(1)}, u32[]{:S(2)}, u32[]{:S(2)}) async-start(bf16[4,256,256]{2,1,0:T(8,128)(2,1)} %broadcast_in_dim.83), calls=%async_computation.12 | async-start | bytes 1048576 | tf_op jit(solution)/shard_map/all_to_all | solution.py:15
  393.1 3.2 collective-permute-start.2
  (2 other events, 2.0 us)

commit v2 on v1

--- a/solution.py
+++ b/solution.py
@@ -17,6 +17,11 @@
 
 def spread(value, axis):
     return swap(jnp.broadcast_to(value[None], (lax.axis_size(axis), *value.shape)), axis)
+
+
+def shifted(value, distance):
+    size = lax.axis_size(TP)
+    return lax.ppermute(value, TP, [(i, (i + distance) % size) for i in range(size)])
 
 
 def in_two(value):
@@ -66,14 +71,37 @@
 
     rows = hidden // pieces
     strip = lax.dynamic_slice_in_dim(w_shared, lax.axis_index(SEQ) * rows, rows, 0)
-    strip = strip.T.reshape(per, hi, rows).transpose(1, 0, 2)
-    own = swap(strip, "tp_hi").reshape(here, rows)
-    w_bc = spread(own, SEQ).transpose(1, 0, 2).reshape(here, hidden)
-
-    def mixer(resid):
+    strip = strip.T.reshape(per, hi, rows // 128, 128).transpose(1, 2, 0, 3)
+    strip = strip.reshape(hi, rows // 128 * per, 128)
+    lo_rank = lax.axis_index("tp_lo")
+
+    def all_columns(own):
+        same = spread(own, "seq_0")
+        other = lax.ppermute(same, "seq_1", [(0, 1), (1, 0)])
+        first = jnp.where(core == 0, same, other)
+        second = jnp.where(core == 0, other, same)
+        both = jnp.stack([first, second], axis=1)
+        both = both.reshape(chips, 2, hi, rows // 128, per, 128).transpose(2, 4, 0, 1, 3, 5)
+        return both.reshape(here, hidden)
+
+    def from_near(far):
+        half = far.shape[1] // 2
+        after = shifted(far, 1)
+        ahead = shifted(far, -1)
+        opposite = jnp.concatenate([shifted(far[:, :half], 2), shifted(far[:, half:], -2)], axis=1)
+        turn = jnp.stack([far, ahead, opposite, after] * 2)
+        return lax.dynamic_slice_in_dim(turn, (lo - lo_rank) % lo, lo, 0)
+
+    def mixer(resid, w_bc):
         count = resid.shape[0]
-        far = spread(resid, "tp_hi")
-        near = spread(far, "tp_lo")
+        sent = jnp.broadcast_to(resid[None], (hi, *resid.shape))
+        if w_bc is None:
+            got = swap(jnp.concatenate([sent, strip], axis=1), "tp_hi")
+            far = got[:, :count]
+            w_bc = all_columns(got[:, count:])
+        else:
+            far = swap(sent, "tp_hi")
+        near = from_near(far)
         values = near.transpose(2, 1, 0, 3).reshape(count, hidden).astype(F32)
         scaled = (values * gain[None, :]).astype(BF)
         inv = lax.rsqrt(jnp.sum(values * values, axis=1, keepdims=True) / hidden + 1e-05)
@@ -85,7 +113,10 @@
 
         cum = jnp.cumsum(-(step * rates[None, :]), axis=0)
         total = cum[count - 1]
-        totals = spread(jnp.broadcast_to(total[:, None], (heads, 128)), SEQ)[:, :, 0]
+        twin = lax.ppermute(jnp.broadcast_to(total[None], (8, heads)), "seq_1", [(0, 1), (1, 0)])[0]
+        pair = jnp.where(core == 0, jnp.stack([total, twin]), jnp.stack([twin, total]))
+        notes = jnp.repeat(jnp.concatenate(in_two(pair)), HEAD_DIM, axis=1)
+        notes = jnp.pad(notes, ((0, 12), (0, 0)))
 
         shared = spread(share, "tp_lo")
         half = here // 2
@@ -96,18 +127,19 @@
         tail = jnp.exp(total[None, :] - cum)
         pushed = (xdt * tail[:, :, None]).reshape(count, channels).astype(BF)
         local = dot(bmat, pushed, ((0,), (0,)))
-        states = spread(local.astype(BF), "seq_0").astype(F32)
+        got = spread(jnp.concatenate([local.astype(BF), notes]), "seq_0").astype(F32)
+        depth = local.shape[0]
+        states = got[:, :depth]
+        totals = (got[:, depth : depth + 2] + got[:, depth + 2 : depth + 4]).reshape(pieces, channels)
 
         edges = jnp.cumsum(totals, axis=0)
         first = lax.dynamic_index_in_dim(edges - totals, 2 * chip, 0, keepdims=True)
         reach = jnp.where(
             jnp.arange(pieces)[:, None] < 2 * chip, jnp.exp(jnp.minimum(first - edges, 0.0)), 0.0
         )
-        mine = lax.dynamic_index_in_dim(reach.reshape(chips, 2, heads), core, 1, keepdims=False)
-        mine = jnp.repeat(mine, HEAD_DIM, axis=1)
+        mine = lax.dynamic_index_in_dim(reach.reshape(chips, 2, channels), core, 1, keepdims=False)
         before = jnp.sum(states * mine[:, None, :], axis=0)
         across = jnp.exp(lax.dynamic_index_in_dim(totals, 2 * chip, 0, keepdims=True))
-        across = jnp.repeat(across, HEAD_DIM, axis=1)
         sent = jnp.where(core == 0, before * across + local, before)
         other = lax.ppermute(sent.astype(BF), "seq_1", [(0, 1), (1, 0)]).astype(F32)
         entering = jnp.where(core == 0, before, before * across) + other
@@ -141,13 +173,13 @@
         summed = jnp.sum(got[:, : hi * count].astype(F32), axis=0).reshape(hi, count, width)
         summed = (summed * unit[None, :, None]).astype(BF)
         summed = jnp.sum(swap(summed, "tp_hi").astype(F32), axis=0)
-        return (resid.astype(F32) + summed).astype(BF)
-
-    opening = mixer(waiting_batchlets[0])
+        return (resid.astype(F32) + summed).astype(BF), w_bc
+
+    opening, w_bc = mixer(waiting_batchlets[0], None)
     sections = lax.axis_size("section")
     moved = lax.ppermute(opening, "section", [(i, i + 1) for i in range(sections - 1)])
     second_in = jnp.where(lax.axis_index("section") == 0, arriving_batchlet, moved)
-    return mixer(second_in)[None]
+    return mixer(second_in, w_bc)[0][None]
 
 
 def solution(mesh, cut=None):

time: 485 us -> 445 us (0.918)
  blocking collectives: 250 us -> 200 us
  starting transfers between devices: 69.6 us -> 93 us
  waiting for transfers between devices: 92.5 us -> 70.8 us
  other arithmetic: 13 us -> 21.6 us
    all_to_all x7 -> x6, blocking collectives: 250 us -> 200 us  [swap(): return lax.all_to_all(value, axis, 0, 0, tiled=True)]
    ppermute x0 -> x11, starting transfers between devices: none -> 42.7 us  [the longest x8 36.8 us: shifted(): lax.ppermute(value, TP, [(i, (i + distance) % size) for i in range(size)])]
    all_to_all x9 -> x5, waiting for transfers between devices: 87.8 us -> 53.9 us  [swap(): return lax.all_to_all(value, axis, 0, 0, tiled=True)]
    all_to_all x9 -> x5, starting transfers between devices: 64.5 us -> 45.2 us  [swap(): return lax.all_to_all(value, axis, 0, 0, tiled=True)]
    ppermute x0 -> x11, waiting for transfers between devices: none -> 12.5 us  [the longest x8 12.1 us: shifted(): lax.ppermute(value, TP, [(i, (i + distance) % size) for i in range(size)])]
  transfers between devices with their start and end apart: 12 -> 19, of which waited for: 10 -> 11; matrix products, arithmetic and copies ran while one was open for 6% -> 7% of each run, Pallas kernels for 0% -> 0%
where the time goes in v2:
time: 445 us; the launch traced here: 436 us
  blocking collectives  200 us (45%)
  starting transfers between devices  93 us (21%)
  waiting for transfers between devices  70.8 us (16%)
  local copies, waits for them, and re-layouts  32.9 us (7%)
  other arithmetic  21.6 us (5%)
  matrix products  17.4 us (4%)
    all_to_all x6, blocking collectives, swap(): return lax.all_to_all(value, axis, 0, 0, tiled=True)  200 us
    all_to_all x5, waiting for transfers between devices, swap(): return lax.all_to_all(value, axis, 0, 0, tiled=True)  53.9 us
    all_to_all x5, starting transfers between devices, swap(): return lax.all_to_all(value, axis, 0, 0, tiled=True)  45.2 us
    ppermute x8, starting transfers between devices, shifted(): lax.ppermute(value, TP, [(i, (i + distance) % size) for i in range(size)])  36.8 us
    dot_general x14, matrix products, dot(): return lax.dot_general(a, b, (dims, ((), ())), preferred_element_type=F32)  14.6 us
    ppermute x8, waiting for transfers between devices, shifted(): lax.ppermute(value, TP, [(i, (i + distance) % size) for i in range(size)])  12.1 us
  transfers between devices with their start and end apart: 19, of which 11 were waited for; matrix products, arithmetic and copies ran while one was open for 7% of the time, Pallas kernels for 0%

profile of v2, /device:TPU:24, one launch (start us, length us, event | category | flops | bytes accessed | tf_op | source)
XLA Modules:
  0.0 436.3 jit_solution(10725226677225410091)
XLA Ops:
  2.8 28.3 %all-to-all-start = ((bf16[8,192,128]{2,1,0:T(8,128)(2,1)}), bf16[8,192,128]{2,1,0:T(8,128)(2,1)S(1)}, u32[]{:S(2)}, u32[]{:S(2)}) async-start(bf16[8,192,128]{2,1,0:T(8,128)(2,1)} %pad_maximum_fusion.2), calls=%async_computation | async-start | bytes 786432 | tf_op jit(solution)/shard_map/all_to_all | solution.py:15
  31.8 39.7 %all-to-all-done = bf16[8,192,128]{2,1,0:T(8,128)(2,1)S(1)} async-done(((bf16[8,192,128]{2,1,0:T(8,128)(2,1)}), bf16[8,192,128]{2,1,0:T(8,128)(2,1)S(1)}, u32[]{:S(2)}, u32[]{:S(2)}) %all-to-all-start) | async-done | bytes 393248 | tf_op jit(solution)/shard_map/all_to_all | solution.py:15
  71.7 12.7 %collective-permute-start.3 = (bf16[8,128,128]{1,2,0:T(8,128)(2,1)S(1)}, bf16[8,128,128]{1,2,0:T(8,128)(2,1)S(1)}, u32[]{:S(2)}, u32[]{:S(2)}) collective-permute-start(bf16[8,128,128]{1,2,0:T(8,128)(2,1)S(1)} %copy.200), channel_id=1, source_target_pairs={{0,1},{1,2},{2,3},{3,4},{4,5},{5,6},{6,7},{7,8},{8,9},{9,10},{10,1... | collective-permute-start | bytes 786440 | tf_op jit(solution)/shard_map/ppermute | solution.py:24
  84.4 1.9 collective-permute-start
  88.6 6.5 %collective-permute-start.2 = (bf16[8,64,128]{1,2,0:T(8,128)(2,1)}, bf16[8,64,128]{1,2,0:T(8,128)(2,1)S(1)}, u32[]{:S(2)}, u32[]{:S(2)}) collective-permute-start(bf16[8,64,128]{1,2,0:T(8,128)(2,1)} %copy.202), channel_id=1, source_target_pairs={{0,30},{1,31},{2,0},{3,1},{4,2},{5,3},{6,4},{7,5},{8,6},{9,7},{10,... | collective-permute-start | bytes 393224 | tf_op jit(solution)/shard_map/ppermute | solution.py:24
  95.2 1.9 collective-permute-start.1
  99.0 4.3 all-to-all-start.1
  103.3 3.0 collective-permute-done.2
  106.4 2.4 collective-permute-done.1
  111.4 1.9 collective-permute-start.4
  115.1 2.9 fusion.10
  125.2 4.9 %all-to-all-start.2 = ((bf16[4,128,128]{1,2,0:T(8,128)(2,1)}), bf16[4,128,128]{1,2,0:T(8,128)(2,1)S(1)}, u32[]{:S(2)}, u32[]{:S(2)}) async-start(bf16[4,128,128]{1,2,0:T(8,128)(2,1)} %broadcast_in_dim.61), calls=%async_computation.2 | async-start | bytes 262144 | tf_op jit(solution)/shard_map/all_to_all | solution.py:15
  132.8 2.1 collective-permute-start.5
  140.7 4.2 all-to-all-start.3
  144.9 10.6 %all-to-all-done.3 = bf16[4,272,256]{2,1,0:T(8,128)(2,1)} async-done(((bf16[4,272,256]{2,1,0:T(8,128)(2,1)}), bf16[4,272,256]{2,1,0:T(8,128)(2,1)}, u32[]{:S(2)}, u32[]{:S(2)}) %all-to-all-start.3) | async-done | bytes 557088 | tf_op jit(solution)/shard_map/all_to_all | solution.py:15
  175.9 2.6 reshape.333
  180.3 31.6 %all_to_all.55 = bf16[4,1040,128]{2,1,0:T(8,128)(2,1)S(1)} all-to-all(bf16[4,1040,128]{2,1,0:T(8,128)(2,1)S(1)} %pad_maximum_fusion), channel_id=1, replica_groups=mesh['section'=4,'seq_0'=4,'seq_1'=2,'tp_hi'=8,'tp_lo'=4] {'tp_lo'}, dimensions={0} | all-to-all | bytes 2129920 | tf_op jit(solution)/shard_map/all_to_all | solution.py:15
  212.2 36.5 %all_to_all.56 = bf16[8,128,128]{2,1,0:T(8,128)(2,1)S(1)} all-to-all(bf16[8,128,128]{2,1,0:T(8,128)(2,1)S(1)} %multiply_convert_fusion.1), channel_id=1, replica_groups=mesh['section'=4,'seq_0'=4,'seq_1'=2,'tp_hi'=8,'tp_lo'=4] {'tp_hi'}, dimensions={0} | all-to-all | bytes 524288 | tf_op jit(solution)/shard_map/all_to_all | solution.py:15
  250.0 4.5 %collective-permute-done.7 = bf16[128,128]{1,0:T(8,128)(2,1)S(1)} collective-permute-done((bf16[128,128]{1,0:T(8,128)(2,1)S(1)}, bf16[128,128]{1,0:T(8,128)(2,1)S(1)}, u32[]{:S(2)}, u32[]{:S(2)}) %collective-permute-start.7) | collective-permute-done | bytes 32800 | tf_op jit(solution)/shard_map/ppermute | solution.py:180
  254.7 51.6 %all_to_all.57 = bf16[8,128,128]{1,2,0:T(8,128)(2,1)S(1)} all-to-all(bf16[8,128,128]{1,2,0:T(8,128)(2,1)S(1)} %broadcast_in_dim.67), channel_id=1, replica_groups=mesh['section'=4,'seq_0'=4,'seq_1'=2,'tp_hi'=8,'tp_lo'=4] {'tp_hi'}, dimensions={0} | all-to-all | bytes 524288 | tf_op jit(solution)/shard_map/all_to_all | solution.py:15
  308.4 2.8 collective-permute-start.9
  311.2 5.2 %collective-permute-start.10 = (bf16[8,64,128]{1,2,0:T(8,128)(2,1)S(1)}, bf16[8,64,128]{1,2,0:T(8,128)(2,1)S(1)}, u32[]{:S(2)}, u32[]{:S(2)}) collective-permute-start(bf16[8,64,128]{1,2,0:T(8,128)(2,1)S(1)} %get-tuple-element.19), channel_id=1, source_target_pairs={{0,30},{1,31},{2,0},{3,1},{4,2},{5,3},{6,4},{7,5},{8,6},{9,7},{10,... | collective-permute-start | bytes 393224 | tf_op jit(solution)/shard_map/ppermute | solution.py:24
  316.4 3.9 collective-permute-start.11
  321.2 2.9 collective-permute-done.10
  324.3 2.9 collective-permute-done.11
  331.7 3.5 all-to-all-start.7
  335.3 1.9 collective-permute-start.12
  338.6 2.3 all-to-all-done.7
  342.5 10.6 %all_to_all.58 = bf16[4,272,256]{2,1,0:T(8,128)(2,1)S(1)} all-to-all(bf16[4,272,256]{2,1,0:T(8,128)(2,1)S(1)} %broadcast_in_dim.71), channel_id=1, replica_groups=mesh['section'=4,'seq_0'=4,'seq_1'=2,'tp_hi'=8,'tp_lo'=4] {'seq_0'}, dimensions={0} | all-to-all | bytes 1114112 | tf_op jit(solution)/shard_map/all_to_all | solution.py:15
  355.1 1.9 collective-permute-start.13
  366.1 31.3 %all_to_all.59 = bf16[4,1040,128]{2,1,0:T(8,128)(2,1)S(1)} all-to-all(bf16[4,1040,128]{2,1,0:T(8,128)(2,1)S(1)} %pad_maximum_fusion.1), channel_id=1, replica_groups=mesh['section'=4,'seq_0'=4,'seq_1'=2,'tp_hi'=8,'tp_lo'=4] {'tp_lo'}, dimensions={0} | all-to-all | bytes 2129920 | tf_op jit(solution)/shard_map/all_to_all | solution.py:15
  397.7 37.9 %all_to_all.60 = bf16[8,128,128]{2,1,0:T(8,128)(2,1)S(1)} all-to-all(bf16[8,128,128]{2,1,0:T(8,128)(2,1)S(1)} %multiply_convert_fusion), channel_id=1, replica_groups=mesh['section'=4,'seq_0'=4,'seq_1'=2,'tp_hi'=8,'tp_lo'=4] {'tp_hi'}, dimensions={0} | all-to-all | bytes 524288 | tf_op jit(solution)/shard_map/all_to_all | solution.py:15
  (210 shorter events, 73.9 us)
Async XLA Ops:
  0.0 174.5 %copy-start = (bf16[1,256,4096]{2,1,0:T(8,128)(2,1)S(1)}, bf16[1,256,4096]{2,1,0:T(8,128)(2,1)}, u32[]{:S(2)}) copy-start(bf16[1,256,4096]{2,1,0:T(8,128)(2,1)} %param.21) | copy-start | bytes 6291460
  0.0 31.2 %copy-start.18 = (s32[1,4]{1,0:T(1,128)S(1)}, s32[1,4]{1,0:T(1,128)}, u32[]{:S(2)}) copy-start(s32[1,4]{1,0:T(1,128)} %param.17) | copy-start | bytes 52
  2.8 68.6 %all-to-all-start = ((bf16[8,192,128]{2,1,0:T(8,128)(2,1)}), bf16[8,192,128]{2,1,0:T(8,128)(2,1)S(1)}, u32[]{:S(2)}, u32[]{:S(2)}) async-start(bf16[8,192,128]{2,1,0:T(8,128)(2,1)} %pad_maximum_fusion.2), calls=%async_computation | async-start | bytes 786432 | tf_op jit(solution)/shard_map/all_to_all | solution.py:15
  71.7 37.3 %collective-permute-start.3 = (bf16[8,128,128]{1,2,0:T(8,128)(2,1)S(1)}, bf16[8,128,128]{1,2,0:T(8,128)(2,1)S(1)}, u32[]{:S(2)}, u32[]{:S(2)}) collective-permute-start(bf16[8,128,128]{1,2,0:T(8,128)(2,1)S(1)} %copy.200), channel_id=1, source_target_pairs={{0,1},{1,2},{2,3},{3,4},{4,5},{5,6},{6,7},{7,8},{8,9},{9,10},{10,1... | collective-permute-start | bytes 786440 | tf_op jit(solution)/shard_map/ppermute | solution.py:24
  84.4 18.9 %collective-permute-start = (bf16[8,128,128]{1,2,0:T(8,128)(2,1)S(1)}, bf16[8,128,128]{1,2,0:T(8,128)(2,1)S(1)}, u32[]{:S(2)}, u32[]{:S(2)}) collective-permute-start(bf16[8,128,128]{1,2,0:T(8,128)(2,1)S(1)} %copy.200), channel_id=1, source_target_pairs={{0,31},{1,0},{2,1},{3,2},{4,3},{5,4},{6,5},{7,6},{8,7},{9,8},{10,9... | collective-permute-start | bytes 786440 | tf_op jit(solution)/shard_map/ppermute | solution.py:24
  88.6 17.7 %collective-permute-start.2 = (bf16[8,64,128]{1,2,0:T(8,128)(2,1)}, bf16[8,64,128]{1,2,0:T(8,128)(2,1)S(1)}, u32[]{:S(2)}, u32[]{:S(2)}) collective-permute-start(bf16[8,64,128]{1,2,0:T(8,128)(2,1)} %copy.202), channel_id=1, source_target_pairs={{0,30},{1,31},{2,0},{3,1},{4,2},{5,3},{6,4},{7,5},{8,6},{9,7},{10,... | collective-permute-start | bytes 393224 | tf_op jit(solution)/shard_map/ppermute | solution.py:24
  95.2 13.6 %collective-permute-start.1 = (bf16[8,64,128]{1,2,0:T(8,128)(2,1)}, bf16[8,64,128]{1,2,0:T(8,128)(2,1)S(1)}, u32[]{:S(2)}, u32[]{:S(2)}) collective-permute-start(bf16[8,64,128]{1,2,0:T(8,128)(2,1)} %copy.201), channel_id=1, source_target_pairs={{0,2},{1,3},{2,4},{3,5},{4,6},{5,7},{6,8},{7,9},{8,10},{9,11},{10,... | collective-permute-start | bytes 393224 | tf_op jit(solution)/shard_map/ppermute | solution.py:24
  99.0 12.5 %all-to-all-start.1 = ((bf16[4,8,64,128]{3,2,1,0:T(8,128)(2,1)}), bf16[4,8,64,128]{3,2,1,0:T(8,128)(2,1)}, u32[]{:S(2)}, u32[]{:S(2)}) async-start(bf16[4,8,64,128]{3,2,1,0:T(8,128)(2,1)} %broadcast_in_dim.60), calls=%async_computation.1 | async-start | bytes 1048576 | tf_op jit(solution)/shard_map/all_to_all | solution.py:15
  103.3 6.1 %copy-start.9 = (f32[1,4096]{1,0:T(1,128)S(1)}, f32[1,4096]{1,0:T(1,128)}, u32[]{:S(2)}) copy-start(f32[1,4096]{1,0:T(1,128)} %param.13) | copy-start | bytes 49156
  110.1 7.9 %copy-start.2 = (bf16[128,8,4,128]{0,3,2,1:T(8,128)(2,1)}, bf16[128,8,4,128]{0,3,2,1:T(8,128)(2,1)S(1)}, u32[]{:S(2)}) copy-start(bf16[128,8,4,128]{0,3,2,1:T(8,128)(2,1)S(1)} %get-tuple-element.12) | copy-start | bytes 3145732
  111.4 6.6 %collective-permute-start.4 = (bf16[4,8,64,128]{3,2,1,0:T(8,128)(2,1)}, bf16[4,8,64,128]{3,2,1,0:T(8,128)(2,1)}, u32[]{:S(2)}, u32[]{:S(2)}) collective-permute-start(bf16[4,8,64,128]{3,2,1,0:T(8,128)(2,1)} %all-to-all-done.1), channel_id=1, source_target_pairs={{0,32},{32,0},{1,33},{33,1},{2,34},{34,2},{3,35},{35,3},{4,36},{36... | collective-permute-start | bytes 1572872 | tf_op jit(solution)/shard_map/ppermute | solution.py:80
  125.2 13.1 %all-to-all-start.2 = ((bf16[4,128,128]{1,2,0:T(8,128)(2,1)}), bf16[4,128,128]{1,2,0:T(8,128)(2,1)S(1)}, u32[]{:S(2)}, u32[]{:S(2)}) async-start(bf16[4,128,128]{1,2,0:T(8,128)(2,1)} %broadcast_in_dim.61), calls=%async_computation.2 | async-start | bytes 262144 | tf_op jit(solution)/shard_map/all_to_all | solution.py:15
  132.8 4.6 %collective-permute-start.5 = (f32[8,4]{1,0:T(8,128)S(1)}, f32[8,4]{1,0:T(8,128)S(1)}, u32[]{:S(2)}, u32[]{:S(2)}) collective-permute-start(f32[8,4]{1,0:T(8,128)S(1)} %broadcast_in_dim.62), channel_id=1, source_target_pairs={{0,32},{32,0},{1,33},{33,1},{2,34},{34,2},{3,35},{35,3},{4,36},{36... | collective-permute-start | bytes 392 | tf_op jit(solution)/shard_map/ppermute | solution.py:116
  140.7 14.8 %all-to-all-start.3 = ((bf16[4,272,256]{2,1,0:T(8,128)(2,1)}), bf16[4,272,256]{2,1,0:T(8,128)(2,1)}, u32[]{:S(2)}, u32[]{:S(2)}) async-start(bf16[4,272,256]{2,1,0:T(8,128)(2,1)} %broadcast_in_dim.64), calls=%async_computation.3 | async-start | bytes 1114112 | tf_op jit(solution)/shard_map/all_to_all | solution.py:15
  144.9 12.9 %copy-start.14 = (pred[4,1]{0,1:T(4,128)(4,1)}, pred[4,1]{0,1:T(4,128)(4,1)S(1)}, u32[]{:S(2)}) copy-start(pred[4,1]{0,1:T(4,128)(4,1)S(1)} %constant_dynamic-slice_fusion.5) | copy-start | bytes 16
  160.9 10.1 %collective-permute-start.6 = (bf16[256,256]{1,0:T(8,128)(2,1)}, bf16[256,256]{1,0:T(8,128)(2,1)}, u32[]{:S(2)}, u32[]{:S(2)}) collective-permute-start(bf16[256,256]{1,0:T(8,128)(2,1)} %fusion.32), channel_id=1, source_target_pairs={{0,32},{32,0},{1,33},{33,1},{2,34},{34,2},{3,35},{35,3},{4,36},{36... | collective-permute-start | bytes 393224 | tf_op jit(solution)/shard_map/ppermute | solution.py:144
  211.9 36.8 %copy-start.8 = (bf16[1,128,128]{2,1,0:T(8,128)(2,1)S(1)}, bf16[1,128,128]{2,1,0:T(8,128)(2,1)}, u32[]{:S(2)}) copy-start(bf16[1,128,128]{2,1,0:T(8,128)(2,1)} %param.11) | copy-start | bytes 98308
  211.9 42.7 %copy-start.10 = (bf16[128,128]{1,0:T(8,128)(2,1)S(1)}, bf16[128,128]{1,0:T(8,128)(2,1)}, u32[]{:S(2)}) copy-start(bf16[128,128]{1,0:T(8,128)(2,1)} %param.12) | copy-start | bytes 98308
  248.7 5.8 %collective-permute-start.7 = (bf16[128,128]{1,0:T(8,128)(2,1)S(1)}, bf16[128,128]{1,0:T(8,128)(2,1)S(1)}, u32[]{:S(2)}, u32[]{:S(2)}) collective-permute-start(bf16[128,128]{1,0:T(8,128)(2,1)S(1)} %add_convert_fusion.1), channel_id=1, source_target_pairs={{0,256},{256,512},{512,768},{1,257},{257,513},{513,769},{2,258},{2... | collective-permute-start | bytes 98312 | tf_op jit(solution)/shard_map/ppermute | solution.py:180
  254.6 72.7 %copy-start.6 = (bf16[128,128]{1,0:T(8,128)(2,1)}, bf16[128,128]{1,0:T(8,128)(2,1)S(1)}, u32[]{:S(2)}) copy-start(bf16[128,128]{1,0:T(8,128)(2,1)S(1)} %broadcast_select_fusion.2) | copy-start | bytes 98308
  306.3 14.0 %collective-permute-start.8 = (bf16[8,128,128]{1,2,0:T(8,128)(2,1)S(1)}, bf16[8,128,128]{1,2,0:T(8,128)(2,1)S(1)}, u32[]{:S(2)}, u32[]{:S(2)}) collective-permute-start(bf16[8,128,128]{1,2,0:T(8,128)(2,1)S(1)} %all_to_all.57), channel_id=1, source_target_pairs={{0,31},{1,0},{2,1},{3,2},{4,3},{5,4},{6,5},{7,6},{8,7},{9,8},{10,9... | collective-permute-start | bytes 786440 | tf_op jit(solution)/shard_map/ppermute | solution.py:24
  308.4 12.8 %collective-permute-start.9 = (bf16[8,64,128]{1,2,0:T(8,128)(2,1)S(1)}, bf16[8,64,128]{1,2,0:T(8,128)(2,1)S(1)}, u32[]{:S(2)}, u32[]{:S(2)}) collective-permute-start(bf16[8,64,128]{1,2,0:T(8,128)(2,1)S(1)} %get-tuple-element.18), channel_id=1, source_target_pairs={{0,2},{1,3},{2,4},{3,5},{4,6},{5,7},{6,8},{7,9},{8,10},{9,11},{10,... | collective-permute-start | bytes 393224 | tf_op jit(solution)/shard_map/ppermute | solution.py:24
  311.2 12.9 %collective-permute-start.10 = (bf16[8,64,128]{1,2,0:T(8,128)(2,1)S(1)}, bf16[8,64,128]{1,2,0:T(8,128)(2,1)S(1)}, u32[]{:S(2)}, u32[]{:S(2)}) collective-permute-start(bf16[8,64,128]{1,2,0:T(8,128)(2,1)S(1)} %get-tuple-element.19), channel_id=1, source_target_pairs={{0,30},{1,31},{2,0},{3,1},{4,2},{5,3},{6,4},{7,5},{8,6},{9,7},{10,... | collective-permute-start | bytes 393224 | tf_op jit(solution)/shard_map/ppermute | solution.py:24
  316.4 10.8 %collective-permute-start.11 = (bf16[8,128,128]{1,2,0:T(8,128)(2,1)S(1)}, bf16[8,128,128]{1,2,0:T(8,128)(2,1)S(1)}, u32[]{:S(2)}, u32[]{:S(2)}) collective-permute-start(bf16[8,128,128]{1,2,0:T(8,128)(2,1)S(1)} %all_to_all.57), channel_id=1, source_target_pairs={{0,1},{1,2},{2,3},{3,4},{4,5},{5,6},{6,7},{7,8},{8,9},{9,10},{10,1... | collective-permute-start | bytes 786440 | tf_op jit(solution)/shard_map/ppermute | solution.py:24
  329.8 8.1 %copy-start.13 = (f32[128,4]{0,1:T(4,128)}, f32[128,4]{0,1:T(4,128)S(1)}, u32[]{:S(2)}) copy-start(f32[128,4]{0,1:T(4,128)S(1)} %get-tuple-element.45) | copy-start | bytes 6148
  331.7 9.2 %all-to-all-start.7 = ((bf16[4,128,128]{1,2,0:T(8,128)(2,1)}), bf16[4,128,128]{1,2,0:T(8,128)(2,1)S(1)}, u32[]{:S(2)}, u32[]{:S(2)}) async-start(bf16[4,128,128]{1,2,0:T(8,128)(2,1)} %broadcast_in_dim.68), calls=%async_computation.7 | async-start | bytes 262144 | tf_op jit(solution)/shard_map/all_to_all | solution.py:15
  335.3 7.2 %copy-start.5 = (f32[128,512]{0,1:T(8,128)}, f32[128,512]{0,1:T(8,128)S(1)}, u32[]{:S(2)}) copy-start(f32[128,512]{0,1:T(8,128)S(1)} %copy.183) | copy-start | bytes 786436
  335.3 3.1 collective-permute-start.12
  341.6 12.4 %copy-start.15 = (pred[4,1]{0,1:T(4,128)(4,1)S(1)}, pred[4,1]{0,1:T(4,128)(4,1)}, u32[]{:S(2)}) copy-start(pred[4,1]{0,1:T(4,128)(4,1)} %copy-done.14) | copy-start | bytes 16
  353.2 7.7 %copy-start.11 = (pred[128,128]{1,0:T(8,128)(4,1)S(1)}, pred[128,128]{1,0:T(8,128)(4,1)}, u32[]{:S(2)}) copy-start(pred[128,128]{1,0:T(8,128)(4,1)} %iota_compare_fusion.1) | copy-start | bytes 49156
  355.1 4.0 collective-permute-start.13
  397.4 38.3 %copy-start.7 = (bf16[128,128]{1,0:T(8,128)(2,1)S(1)}, bf16[128,128]{1,0:T(8,128)(2,1)}, u32[]{:S(2)}) copy-start(bf16[128,128]{1,0:T(8,128)(2,1)} %copy-done.6) | copy-start | bytes 98308
  (10 other events, 22.9 us)

commit v3 on v2

v3 whole, which is shorter than its diff:
```python
import jax
import jax.numpy as jnp
from jax import lax
from jax.experimental import pallas as pl
from jax.experimental.pallas import tpu as pltpu
from jax.sharding import Mesh
from jax.sharding import PartitionSpec as P

HEAD_DIM = 64
SEQ = ("seq_0", "seq_1")
TP = ("tp_hi", "tp_lo")
BF = jnp.bfloat16
F32 = jnp.float32
EXACT = lax.Precision.HIGHEST
INTERPRET = False


def swap(value, axis):
    return lax.all_to_all(value, axis, 0, 0, tiled=True)


def spread(value, axis):
    return swap(jnp.broadcast_to(value[None], (lax.axis_size(axis), *value.shape)), axis)


def shifted(value, distance):
    size = lax.axis_size(TP)
    return lax.ppermute(value, TP, [(i, (i + distance) % size) for i in range(size)])


def dot(a, b, dims=((1,), (0,))):
    return lax.dot_general(a, b, (dims, ((), ())), preferred_element_type=F32)


def lanes_of(value):
    low = lax.broadcasted_iota(jnp.int32, (value.shape[0], 128), 1) < HEAD_DIM
    return jnp.concatenate(
        [jnp.where(low, value[:, h : h + 1], value[:, h + 1 : h + 2]) for h in (0, 2)], axis=1
    )


def split_pair(a, b):
    low = lax.broadcasted_iota(jnp.int32, a.shape, 1) < 64
    first = jnp.where(low, a, pltpu.roll(b, 64, 1))
    second = jnp.where(low, pltpu.roll(a, 64, 1), b)
    return first, second


def project_kernel(
    place, far, ahead, across_a, across_b, behind, gain, w_inp, same, other, w_step, bias, rates,
    share, x_out, g_out, step_out, cum_out, total_out, order, acc_p, acc_b, acc_s, acc_q,
):
    i = pl.program_id(0)
    lo = order.shape[0]
    me = place[0]
    core = place[1]
    count = order.shape[1]
    half = count // 2

    @pl.when(i == 0)
    def _():
        acc_p[...] = jnp.zeros_like(acc_p)
        acc_b[...] = jnp.zeros_like(acc_b)
        acc_s[...] = jnp.zeros_like(acc_s)
        acc_q[...] = jnp.zeros_like(acc_q)

    order[me] = far[0]
    order[(me + 1) % lo] = ahead[0]
    order[(me + 2) % lo, :half] = across_a[0]
    order[(me + 2) % lo, half:] = across_b[0]
    order[(me + 3) % lo] = behind[0]
    values = jnp.concatenate([order[j] for j in range(lo)], axis=1).astype(F32)
    row = jnp.concatenate([gain[0, j : j + 1] for j in range(lo)], axis=1)
    acc_q[...] += jnp.sum(values * values, axis=1, keepdims=True)
    scaled = (values * row).astype(BF)
    acc_p[...] += dot(scaled, w_inp[...])
    acc_s[...] += dot(scaled, w_step[...])

    def add_share(ref):
        parts = [ref[0, :, j].reshape(128, 128) for j in range(lo)]
        acc_b[...] += dot(scaled, jnp.concatenate(parts, axis=1), ((1,), (1,)))

    @pl.when(i % 2 == core)
    def _():
        add_share(same)

    @pl.when(i % 2 != core)
    def _():
        add_share(other)

    @pl.when(i == pl.num_programs(0) - 1)
    def _():
        inv = lax.rsqrt(acc_q[...] / w_total(w_inp, i) + 1e-05)
        sent = (acc_b[...] * inv).astype(BF)
        for j in range(lo):
            share[j] = sent
        for q in (0, 1):
            left = acc_p[:, 256 * q : 256 * q + 128] * inv
            right = acc_p[:, 256 * q + 128 : 256 * q + 256] * inv
            xs, gates = split_pair(left, right)
            x_out[:, 128 * q : 128 * q + 128] = xs
            g_out[:, 128 * q : 128 * q + 128] = gates
        raw = acc_s[...] * inv + bias[...]
        step = jnp.maximum(raw, 0.0) + jnp.log1p(jnp.exp(-jnp.abs(raw)))
        step_out[...] = step
        shape = (count, count)
        lower = lax.broadcasted_iota(jnp.int32, shape, 0) >= lax.broadcasted_iota(jnp.int32, shape, 1)
        cum = jnp.dot(
            lower.astype(F32), -(step * rates[...]), precision=EXACT, preferred_element_type=F32
        )
        cum_out[...] = cum
        total_out[...] = jnp.broadcast_to(cum[count - 1 : count], total_out.shape)


def w_total(w_inp, i):
    return w_inp.shape[0] * pl.num_programs(0)


def piece_kernel(
    place, shared, x_in, step, cum, twin, skip, sent, local, y_out, c_out, grow
):
    core = place[1]
    count = x_in.shape[0]
    pairs = [
        split_pair(shared[k].astype(F32), shared[k + 1].astype(F32))
        for k in range(0, shared.shape[0], 2)
    ]
    bmat = jnp.concatenate([p[0] for p in pairs], axis=1).astype(BF)
    cmat = jnp.concatenate([p[1] for p in pairs], axis=1).astype(BF)
    c_out[...] = cmat
    scores = dot(cmat, bmat, ((1,), (1,)))
    cums = cum[...]
    turned = cums.T
    xs = x_in[...]
    xdt = xs * lanes_of(step[...])
    total = cums[count - 1 : count]
    pushed = (xdt * lanes_of(jnp.exp(total - cums))).astype(BF)
    states = dot(bmat, pushed, ((0,), (0,)))
    local[...] = states
    xdt = xdt.astype(BF)
    shape = (count, count)
    lower = lax.broadcasted_iota(jnp.int32, shape, 0) >= lax.broadcasted_iota(jnp.int32, shape, 1)
    low = lax.broadcasted_iota(jnp.int32, (count, 128), 1) < HEAD_DIM
    for q in (0, 1):
        block = xdt[:, 128 * q : 128 * q + 128]
        made = []
        for h in (2 * q, 2 * q + 1):
            gap = jnp.minimum(cums[:, h : h + 1] - turned[h : h + 1, :], 0.0)
            mask = jnp.where(lower, jnp.exp(gap), 0.0) * scores
            made.append(dot(mask.astype(BF), block))
        at = slice(128 * q, 128 * q + 128)
        y_out[:, at] = jnp.where(low, made[0], made[1]) + skip[:, at] * xs[:, at]
    grow[...] = lanes_of(jnp.exp(cums))
    mine = lanes_of(total)
    theirs = lanes_of(twin[0:1])
    first = jnp.where(core == 0, mine, theirs)
    second = jnp.where(core == 0, theirs, mine)
    line = lax.broadcasted_iota(jnp.int32, (16, first.shape[1]), 0)
    high_a = first.astype(BF).astype(F32)
    high_b = second.astype(BF).astype(F32)
    notes = jnp.where(line == 0, high_a, 0.0)
    notes = jnp.where(line == 1, high_b, notes)
    notes = jnp.where(line == 2, first - high_a, notes)
    notes = jnp.where(line == 3, second - high_b, notes).astype(BF)
    depth = states.shape[0]
    states = states.astype(BF)
    for k in range(sent.shape[0]):
        sent[k, :depth] = states
        sent[k, depth:] = notes


def carry_kernel(place, got, local, sent, keep):
    core = place[1]
    chip = place[2]
    chips = got.shape[0]
    depth = local.shape[0]
    firsts, seconds = [], []
    for k in range(chips):
        notes = got[k, depth:].astype(F32)
        firsts.append(notes[0:1] + notes[2:3])
        seconds.append(notes[1:2] + notes[3:4])
    until = jnp.zeros_like(firsts[0])
    own = jnp.zeros_like(firsts[0])
    for k in range(chips):
        until = until + jnp.where(k < chip, firsts[k] + seconds[k], 0.0)
        own = own + jnp.where(k == chip, firsts[k], 0.0)
    before = jnp.zeros(local.shape, F32)
    edge = jnp.zeros_like(firsts[0])
    for k in range(chips - 1):
        end = edge + firsts[k] + jnp.where(core == 1, seconds[k], 0.0)
        weight = jnp.where(k < chip, jnp.exp(jnp.minimum(until - end, 0.0)), 0.0)
        before = before + weight * got[k, :depth].astype(F32)
        edge = edge + firsts[k] + seconds[k]
    moved = before * jnp.exp(own)
    sent[...] = jnp.where(core == 0, moved + local[...], before).astype(BF)
    keep[...] = jnp.where(core == 0, before, moved)


def gate_kernel(other, keep, cmat, y_in, grow, g_in, o_gain, sent):
    entering = (keep[...] + other[...].astype(F32)).astype(BF)
    mixed = y_in[...] + dot(cmat[...], entering) * grow[...]
    gates = g_in[...]
    gated = mixed * (gates * lax.logistic(gates))
    squares = gated * gated
    count, width = squares.shape
    part = lax.dot_general(
        jnp.ones((16, width), F32),
        squares,
        (((1,), (1,)), ((), ())),
        precision=EXACT,
        preferred_element_type=F32,
    )
    high = part.astype(BF).astype(F32)
    line = lax.broadcasted_iota(jnp.int32, part.shape, 0)
    notes = jnp.where(line == 0, high, jnp.where(line == 1, part - high, 0.0))
    notes = jnp.concatenate([notes, jnp.zeros((16, width - count), F32)], axis=1).astype(BF)
    out = (gated * o_gain[...]).astype(BF)
    for k in range(sent.shape[0]):
        sent[k, :count] = out
        sent[k, count:] = notes


def close_kernel(got, weight, sent):
    lo = got.shape[0]
    count = sent.shape[1]
    left = jnp.concatenate([got[k, :count] for k in range(lo)], axis=1)
    product = dot(left, weight[...])
    square = jnp.zeros((16, count), F32)
    for k in range(lo):
        square = square + got[k, count:, :count].astype(F32)
    unit = lax.rsqrt((square[0:1] + square[1:2]) / left.shape[1] + 1e-05)
    shape = (count, count)
    same = lax.broadcasted_iota(jnp.int32, shape, 0) == lax.broadcasted_iota(jnp.int32, shape, 1)
    unit = jnp.sum(jnp.where(same, unit, 0.0), axis=1, keepdims=True)
    product = (product * unit).astype(BF)
    for k in range(sent.shape[0]):
        sent[k] = product[:, 128 * k : 128 * k + 128]


SCALARS = pl.BlockSpec(memory_space=pltpu.SMEM)


def whole(shape):
    return pl.BlockSpec(shape, lambda *_: (0,) * len(shape))


def run(kernel, name, args, outs, place=None):
    specs = [whole(a.shape) for a in args]
    if place is not None:
        args, specs = (place, *args), [SCALARS, *specs]
    return pl.pallas_call(
        kernel,
        out_shape=[jax.ShapeDtypeStruct(*o) for o in outs],
        in_specs=specs,
        out_specs=[whole(o[0]) for o in outs],
        interpret=INTERPRET,
        name=name,
    )(*args)


def body(
    waiting_batchlets,
    arriving_batchlet,
    entry_rescale_factor,
    entry_projection_matrix,
    timescale_projection,
    timescale_offset,
    channel_forgetting_rate,
    state_read_write_matrix,
    direct_passthrough,
    closing_rescale_factor,
    closing_projection_matrix,
):
    gain = entry_rescale_factor[0]
    w_inp = entry_projection_matrix[0]
    w_step = timescale_projection[0]
    bias = timescale_offset[0]
    rates = 0.0005 * jnp.exp2(channel_forgetting_rate[0].astype(F32))
    w_shared = state_read_write_matrix[0]
    skip_coef = direct_passthrough[0]
    o_gain = closing_rescale_factor[0]
    w_outp = closing_projection_matrix[0]

    hi = lax.axis_size("tp_hi")
    lo = lax.axis_size("tp_lo")
    pieces = lax.axis_size(SEQ)
    chips = lax.axis_size("seq_0")
    chip = lax.axis_index("seq_0")
    core = lax.axis_index("seq_1")
    hidden = w_inp.shape[0]
    heads = bias.shape[0]
    channels = heads * HEAD_DIM
    group_size = channels * lo
    here = w_shared.shape[1]
    per = here // hi

    rows = hidden // pieces
    strip = lax.dynamic_slice_in_dim(w_shared, lax.axis_index(SEQ) * rows, rows, 0)
    strip = strip.T.reshape(per, hi, rows // 128, 128).transpose(1, 2, 0, 3)
    strip = strip.reshape(hi, rows // 128 * per, 128)
    lo_rank = lax.axis_index("tp_lo")

    def both_cores(same):
        other = lax.ppermute(same, "seq_1", [(0, 1), (1, 0)])
        return same, other

    def turned(parts, rank):
        ring = jnp.stack(parts * 2)
        size = len(parts)
        return lax.dynamic_slice_in_dim(ring, (size - rank) % size, size, 0)

    def from_ring(value, axis, pick):
        size = lax.axis_size(axis)
        parts = [pick(value, 0)]
        for k in range(1, size):
            route = [(i, (i - k) % size) for i in range(size)]
            parts.append(lax.ppermute(pick(value, -k), axis, route))
        return turned(parts, lax.axis_index(axis))

    strip_rows = channels // pieces
    cut = lax.dynamic_slice_in_dim(w_outp, lax.axis_index(SEQ) * strip_rows, strip_rows, 0)
    cut = cut.reshape(strip_rows, hi, lo, 128).transpose(2, 0, 1, 3).reshape(lo, strip_rows, hi * 128)

    def for_peer(value, k):
        return lax.dynamic_index_in_dim(value, (lo_rank + k) % lo, 0, keepdims=False)

    group_rows = from_ring(cut, "tp_lo", for_peer)
    group_rows = from_ring(group_rows, "seq_0", lambda value, k: value)
    same, other = both_cores(group_rows)
    w_out = jnp.stack([jnp.where(core == 0, same, other), jnp.where(core == 0, other, same)])
    w_out = w_out.transpose(2, 1, 0, 3, 4).reshape(group_size, hi * 128)

    place = jnp.stack([lo_rank, core, chip]).astype(jnp.int32)
    gain = gain.reshape(hi, lo, 128)
    w_step = jnp.pad(w_step, ((0, 0), (0, 128 - heads)))
    bias = jnp.pad(bias, (0, 128 - heads))[None]
    rates = jnp.pad(rates, (0, 128 - heads))[None]
    skip = jnp.repeat(skip_coef, HEAD_DIM)[None]
    o_gain = o_gain[None]

    def mixer(resid, w_bc):
        count = resid.shape[0]
        half = count // 2
        sent = jnp.broadcast_to(resid[None], (hi, *resid.shape))
        if w_bc is None:
            got = swap(jnp.concatenate([sent, strip], axis=1), "tp_hi")
            far = got[:, :count]
            own = got[:, count:].reshape(hi, rows // 128, per, 128)
            w_bc = both_cores(spread(own, "seq_0"))
        else:
            far = swap(sent, "tp_hi")
        behind = shifted(far, 1)
        ahead = shifted(far, -1)
        across_a = shifted(far[:, :half], 2)
        across_b = shifted(far[:, half:], -2)

        def by_hi(rows_here):
            return pl.BlockSpec((1, rows_here, 128), lambda i: (i, 0, 0))

        strip_spec = pl.BlockSpec((1, *w_bc[0].shape[1:]), lambda i: (i // 2, 0, 0, 0, 0))
        tall = lo * 128
        outs = [
            ((lo, count, 128), BF),
            ((count, channels), F32),
            ((count, channels), F32),
            ((count, 128), F32),
            ((count, 128), F32),
            ((8, 128), F32),
        ]
        share, xs, gates, step, cum, total = pl.pallas_call(
            project_kernel,
            grid=(hi,),
            out_shape=[jax.ShapeDtypeStruct(*o) for o in outs],
            in_specs=[
                SCALARS,
                by_hi(count),
                by_hi(count),
                by_hi(half),
                by_hi(half),
                by_hi(count),
                pl.BlockSpec((1, lo, 128), lambda i: (i, 0, 0)),
                pl.BlockSpec((tall, w_inp.shape[1]), lambda i: (i, 0)),
                strip_spec,
                strip_spec,
                pl.BlockSpec((tall, 128), lambda i: (i, 0)),
                whole((1, 128)),
                whole((1, 128)),
            ],
            out_specs=[whole(o[0]) for o in outs],
            scratch_shapes=[
                pltpu.VMEM((lo, count, 128), BF),
                pltpu.VMEM((count, w_inp.shape[1]), F32),
                pltpu.VMEM((count, 128), F32),
                pltpu.VMEM((count, 128), F32),
                pltpu.VMEM((count, 1), F32),
            ],
            interpret=INTERPRET,
            name="project",
        )(place, far, ahead, across_a, across_b, behind, gain, w_inp, *w_bc, w_step, bias, rates)

        twin = lax.ppermute(total, "seq_1", [(0, 1), (1, 0)])
        shared = swap(share, "tp_lo")
        depth = lo * here // 2
        sent, local, y, cmat, grow = run(
            piece_kernel,
            "piece",
            (shared, xs, step, cum, twin, skip),
            [
                ((chips, depth + 16, channels), BF),
                ((depth, channels), F32),
                ((count, channels), F32),
                ((count, depth), BF),
                ((count, channels), F32),
            ],
            place,
        )
        got = swap(sent, "seq_0")
        sent, keep = run(
            carry_kernel,
            "carry",
            (got, local),
            [((depth, channels), BF), ((depth, channels), F32)],
            place,
        )
        other = lax.ppermute(sent, "seq_1", [(0, 1), (1, 0)])
        (sent,) = run(
            gate_kernel,
            "gate",
            (other, keep, cmat, y, grow, gates, o_gain),
            [((lo, count + 16, channels), BF)],
        )
        got = swap(sent, "tp_lo")
        shares = pl.pallas_call(
            close_kernel,
            grid=(hi // 2,),
            out_shape=jax.ShapeDtypeStruct((hi, count, 128), BF),
            in_specs=[
                whole(got.shape),
                pl.BlockSpec((group_size, 256), lambda i: (0, i)),
            ],
            out_specs=pl.BlockSpec((2, count, 128), lambda i: (i, 0, 0)),
            interpret=INTERPRET,
            name="close",
        )(got, w_out)
        summed = jnp.sum(swap(shares, "tp_hi").astype(F32), axis=0)
        return (resid.astype(F32) + summed).astype(BF), w_bc

    opening, w_bc = mixer(waiting_batchlets[0], None)
    sections = lax.axis_size("section")
    moved = lax.ppermute(opening, "section", [(i, i + 1) for i in range(sections - 1)])
    second_in = jnp.where(lax.axis_index("section") == 0, arriving_batchlet, moved)
    return mixer(second_in, w_bc)[0][None]


def solution(mesh, cut=None):
    sections, seq, tp = (mesh.shape[name] for name in ("section", "seq", "tp"))
    near = cut or 4
    torus = Mesh(
        mesh.devices.reshape(sections, seq // 2, 2, tp // near, near),
        ("section", *SEQ, *TP),
    )
    return jax.shard_map(
        body,
        mesh=torus,
        in_specs=(
            P("section", SEQ, TP),
            P(SEQ, TP),
            P("section", None),
            P("section", None, TP),
            P("section", None, TP),
            P("section", TP),
            P("section", TP),
            P("section", None, TP),
            P("section", TP),
            P("section", TP),
            P("section", TP, None),
        ),
        out_specs=P("section", SEQ, TP),
        check_vma=False,
    )
```

time: 445 us -> 432 us (0.971)
  Pallas kernels: 0 us -> 39.3 us
  blocking collectives: 200 us -> 161 us
  starting transfers between devices: 93 us -> 121 us
  other arithmetic: 21.6 us -> 3.71 us
  matrix products: 17.4 us -> 0 us
  waiting for transfers between devices: 70.8 us -> 63.5 us
    all_to_all x5 -> x6, waiting for transfers between devices: 53.9 us -> 9.59 us  [swap(): return lax.all_to_all(value, axis, 0, 0, tiled=True)]
    ppermute x5 -> x12, waiting for transfers between devices: 0.4 us -> 42.7 us  [the longest x6 36.2 us: from_ring(): parts.append(lax.ppermute(pick(value, -k), axis, route))]
    pallas_call x0 -> x10, Pallas kernels: none -> 39.3 us  [the longest x2 17.9 us: mixer(): pl.pallas_call(project_kernel, grid=(hi,), out_shape=[jax.ShapeDtypeStruc...]
    all_to_all x6 -> x5, blocking collectives: 200 us -> 161 us  [swap(): return lax.all_to_all(value, axis, 0, 0, tiled=True)]
    ppermute x5 -> x12, starting transfers between devices: 9.77 us -> 31 us  [the longest x6 19.6 us: from_ring(): parts.append(lax.ppermute(pick(value, -k), axis, route))]
    dot_general x16 -> x0, matrix products: 17.4 us -> none  [the longest x14 14.6 us: dot(): return lax.dot_general(a, b, (dims, ((), ())), preferred_element_type=F32)]
    unnamed x60 -> x62, local copies, waits for them, and re-layouts: 4.43 us -> 20.5 us
    reshape x9 -> x2, local copies, waits for them, and re-layouts: 9.45 us -> 0.29 us  [body(): cut.reshape(strip_rows, hi, lo, 128).transpose(2, 0, 1, 3)]
  transfers between devices with their start and end apart: 19 -> 27, of which waited for: 11 -> 14; matrix products, arithmetic and copies ran while one was open for 7% -> 7% of each run, Pallas kernels for 0% -> 2%
where the time goes in v3:
time: 432 us; the launch traced here: 425 us
  blocking collectives  161 us (37%)
  starting transfers between devices  121 us (28%)
  waiting for transfers between devices  63.5 us (15%)
  Pallas kernels  39.3 us (9%)
  local copies, waits for them, and re-layouts  35.7 us (8%)
    all_to_all x5, blocking collectives, swap(): return lax.all_to_all(value, axis, 0, 0, tiled=True)  161 us
    all_to_all x6, starting transfers between devices, swap(): return lax.all_to_all(value, axis, 0, 0, tiled=True)  49.4 us
    ppermute x8, starting transfers between devices, shifted(): lax.ppermute(value, TP, [(i, (i + distance) % size) for i in range(size)])  39.3 us
    ppermute x6, waiting for transfers between devices, from_ring(): parts.append(lax.ppermute(pick(value, -k), axis, route))  36.2 us
    unnamed x62, local copies, waits for them, and re-layouts  20.5 us
    ppermute x6, starting transfers between devices, from_ring(): parts.append(lax.ppermute(pick(value, -k), axis, route))  19.6 us
    pallas_call x2, Pallas kernels, mixer(): pl.pallas_call(project_kernel, grid=(hi,), out_shape=[jax.ShapeDtypeStruc...  17.9 us
    pallas_call x6, Pallas kernels, run(): pl.pallas_call(kernel, out_shape=[jax.ShapeDtypeStruct(*o) for o in outs]...  13.6 us
  transfers between devices with their start and end apart: 27, of which 14 were waited for; matrix products, arithmetic and copies ran while one was open for 7% of the time, Pallas kernels for 2%

profile of v3, /device:TPU:24, one launch (start us, length us, event | category | flops | bytes accessed | tf_op | source)
XLA Modules:
  0.0 425.2 jit_solution(16500262501944413953)
XLA Ops:
  2.8 28.3 %all-to-all-start = ((bf16[8,192,128]{2,1,0:T(8,128)(2,1)}), bf16[8,192,128]{2,1,0:T(8,128)(2,1)S(1)}, u32[]{:S(2)}, u32[]{:S(2)}) async-start(bf16[8,192,128]{2,1,0:T(8,128)(2,1)} %pad_maximum_fusion), calls=%async_computation | async-start | bytes 786432 | tf_op jit(solution)/shard_map/all_to_all | solution.py:19
  32.2 3.8 collective-permute-start.7
  38.5 2.9 collective-permute-start.9
  41.5 22.8 %collective-permute-done.7 = bf16[32,1024]{1,0:T(8,128)(2,1)S(1)} collective-permute-done((bf16[32,1024]{1,0:T(8,128)(2,1)S(1)}, bf16[32,1024]{1,0:T(8,128)(2,1)S(1)}, u32[]{:S(2)}, u32[]{:S(2)}) %collective-permute-start.7) | collective-permute-done | bytes 65568 | tf_op jit(solution)/shard_map/ppermute | solution.py:317
  64.9 6.7 %collective-permute-done.8 = bf16[32,1024]{1,0:T(8,128)(2,1)S(1)} collective-permute-done((bf16[32,1024]{1,0:T(8,128)(2,1)S(1)}, bf16[32,1024]{1,0:T(8,128)(2,1)S(1)}, u32[]{:S(2)}, u32[]{:S(2)}) %collective-permute-start.8) | collective-permute-done | bytes 65568 | tf_op jit(solution)/shard_map/ppermute | solution.py:317
  75.7 4.3 %all-to-all-start.1 = ((bf16[4,8,4,16,128]{4,3,2,1,0:T(8,128)(2,1)}), bf16[4,8,4,16,128]{4,3,2,1,0:T(8,128)(2,1)S(1)}, u32[]{:S(2)}, u32[]{:S(2)}) async-start(bf16[4,8,4,16,128]{4,3,2,1,0:T(8,128)(2,1)} %broadcast_in_dim.32), calls=%async_computation.1 | async-start | bytes 1048576 | tf_op jit(solution)/shard_map/all_to_all | solution.py:19
  81.3 15.3 %collective-permute-start.1 = (bf16[8,64,128]{2,1,0:T(8,128)(2,1)}, bf16[8,64,128]{2,1,0:T(8,128)(2,1)}, u32[]{:S(2)}, u32[]{:S(2)}) collective-permute-start(bf16[8,64,128]{2,1,0:T(8,128)(2,1)} %get-tuple-element.63), channel_id=1, source_target_pairs={{0,2},{1,3},{2,4},{3,5},{4,6},{5,7},{6,8},{7,9},{8,10},{9,11},{10,... | collective-permute-start | bytes 393224 | tf_op jit(solution)/shard_map/ppermute | solution.py:28
  102.8 3.9 collective-permute-start.3
  108.6 5.1 %collective-permute-start.10 = (bf16[4,32,1024]{2,1,0:T(8,128)(2,1)}, bf16[4,32,1024]{2,1,0:T(8,128)(2,1)S(1)}, u32[]{:S(2)}, u32[]{:S(2)}) collective-permute-start(bf16[4,32,1024]{2,1,0:T(8,128)(2,1)} %get-tuple-element.58), channel_id=1, source_target_pairs={{0,192},{64,0},{128,64},{192,128},{1,193},{65,1},{129,65},{193,129... | collective-permute-start | bytes 786440 | tf_op jit(solution)/shard_map/ppermute | solution.py:317
  113.7 4.2 collective-permute-start.2
  125.9 9.0 %project.2 = (bf16[4,128,128]{2,1,0:T(8,128)(2,1)}, f32[128,256]{1,0:T(8,128)}, f32[128,256]{1,0:T(8,128)}, f32[128,128]{1,0:T(8,128)}, f32[128,128]{1,0:T(8,128)}, /*index=5*/f32[8,128]{1,0:T(8,128)}) custom-call(s32[3]{0:T(128)} %pad_add_fusion.place, bf16[8,128,128]{2,1,0:T(8,128)(2,1)} %slice.26.far, bf16[8,128,128]{2,1,0:T(8,128)(2,1)} %collective-permute-done.ahead, ...), custom_call_target="tpu_custom_call" | custom-call | tf_op jit(solution)/shard_map/project/pallas_call | solution.py:370
  134.9 5.1 %all-to-all-start.2 = ((bf16[4,128,128]{2,1,0:T(8,128)(2,1)}), bf16[4,128,128]{2,1,0:T(8,128)(2,1)S(1)}, u32[]{:S(2)}, u32[]{:S(2)}) async-start(bf16[4,128,128]{2,1,0:T(8,128)(2,1)} %get-tuple-element.31), calls=%async_computation.2 | async-start | bytes 262144 | tf_op jit(solution)/shard_map/all_to_all | solution.py:19
  140.0 3.3 collective-permute-start.11
  146.9 5.5 %collective-permute-done.11 = bf16[4,32,1024]{2,1,0:T(8,128)(2,1)S(1)} collective-permute-done((bf16[4,32,1024]{2,1,0:T(8,128)(2,1)}, bf16[4,32,1024]{2,1,0:T(8,128)(2,1)S(1)}, u32[]{:S(2)}, u32[]{:S(2)}) %collective-permute-start.11) | collective-permute-done | bytes 262176 | tf_op jit(solution)/shard_map/ppermute | solution.py:317
  160.1 3.5 all-to-all-start.3
  166.9 6.4 %all-to-all-done.3.got = bf16[4,272,256]{2,1,0:T(8,128)(2,1)S(1)} async-done(((bf16[4,272,256]{2,1,0:T(8,128)(2,1)}), bf16[4,272,256]{2,1,0:T(8,128)(2,1)S(1)}, u32[]{:S(2)}, u32[]{:S(2)}) %all-to-all-start.3) | async-done | bytes 557088 | tf_op jit(solution)/shard_map/all_to_all | solution.py:19
  182.6 4.8 %all-to-all-start.4 = ((bf16[4,144,256]{2,1,0:T(8,128)(2,1)}), bf16[4,144,256]{2,1,0:T(8,128)(2,1)S(1)}, u32[]{:S(2)}, u32[]{:S(2)}) async-start(bf16[4,144,256]{2,1,0:T(8,128)(2,1)} %gate.2), calls=%async_computation.4 | async-start | bytes 589824 | tf_op jit(solution)/shard_map/all_to_all | solution.py:19
  192.3 2.8 collective-permute-done.13
  199.0 3.9 close.2
  202.9 42.6 %all_to_all.55 = bf16[8,128,128]{2,1,0:T(8,128)(2,1)S(1)} all-to-all(bf16[8,128,128]{2,1,0:T(8,128)(2,1)} %close.2), channel_id=1, replica_groups=mesh['section'=4,'seq_0'=4,'seq_1'=2,'tp_hi'=8,'tp_lo'=4] {'tp_hi'}, dimensions={0} | all-to-all | bytes 524288 | tf_op jit(solution)/shard_map/all_to_all | solution.py:19
  246.9 4.5 %collective-permute-done.14 = bf16[128,128]{1,0:T(8,128)(2,1)S(1)} collective-permute-done((bf16[128,128]{1,0:T(8,128)(2,1)S(1)}, bf16[128,128]{1,0:T(8,128)(2,1)S(1)}, u32[]{:S(2)}, u32[]{:S(2)}) %collective-permute-start.14) | collective-permute-done | bytes 32800 | tf_op jit(solution)/shard_map/ppermute | solution.py:450
  251.4 51.5 %all_to_all.56.far = bf16[8,128,128]{2,1,0:T(8,128)(2,1)S(1)} all-to-all(bf16[8,128,128]{2,1,0:T(8,128)(2,1)S(1)} %broadcast_in_dim.36), channel_id=1, replica_groups=mesh['section'=4,'seq_0'=4,'seq_1'=2,'tp_hi'=8,'tp_lo'=4] {'tp_hi'}, dimensions={0} | all-to-all | bytes 524288 | tf_op jit(solution)/shard_map/all_to_all | solution.py:19
  304.8 3.9 collective-permute-start.18
  308.8 4.3 %collective-permute-start.16 = (bf16[8,64,128]{2,1,0:T(8,128)(2,1)S(1)}, bf16[8,64,128]{2,1,0:T(8,128)(2,1)S(1)}, u32[]{:S(2)}, u32[]{:S(2)}) collective-permute-start(bf16[8,64,128]{2,1,0:T(8,128)(2,1)S(1)} %get-tuple-element.65), channel_id=1, source_target_pairs={{0,2},{1,3},{2,4},{3,5},{4,6},{5,7},{6,8},{7,9},{8,10},{9,11},{10,... | collective-permute-start | bytes 393224 | tf_op jit(solution)/shard_map/ppermute | solution.py:28
  313.1 3.6 collective-permute-start.17
  316.8 5.3 %collective-permute-done.16.across_a = bf16[8,64,128]{2,1,0:T(8,128)(2,1)S(1)} collective-permute-done((bf16[8,64,128]{2,1,0:T(8,128)(2,1)S(1)}, bf16[8,64,128]{2,1,0:T(8,128)(2,1)S(1)}, u32[]{:S(2)}, u32[]{:S(2)}) %collective-permute-start.16) | collective-permute-done | bytes 131104 | tf_op jit(solution)/shard_map/ppermute | solution.py:28
  323.5 8.9 %project.3 = (bf16[4,128,128]{2,1,0:T(8,128)(2,1)}, f32[128,256]{1,0:T(8,128)}, f32[128,256]{1,0:T(8,128)}, f32[128,128]{1,0:T(8,128)}, f32[128,128]{1,0:T(8,128)}, /*index=5*/f32[8,128]{1,0:T(8,128)}) custom-call(s32[3]{0:T(128)} %pad_add_fusion.place, bf16[8,128,128]{2,1,0:T(8,128)(2,1)} %copy-done.2, bf16[8,128,128]{2,1,0:T(8,128)(2,1)} %copy-done.9, ...), custom_call_target="tpu_custom_call" | custom-call | tf_op jit(solution)/shard_map/project/pallas_call | solution.py:370
  332.5 3.3 all-to-all-start.7
  344.8 12.5 %all_to_all.57.got = bf16[4,272,256]{2,1,0:T(8,128)(2,1)} all-to-all(bf16[4,272,256]{2,1,0:T(8,128)(2,1)} %get-tuple-element.49), channel_id=1, replica_groups=mesh['section'=4,'seq_0'=4,'seq_1'=2,'tp_hi'=8,'tp_lo'=4] {'seq_0'}, dimensions={0} | all-to-all | bytes 1114112 | tf_op jit(solution)/shard_map/all_to_all | solution.py:19
  365.7 14.6 %all_to_all.58.got = bf16[4,144,256]{2,1,0:T(8,128)(2,1)} all-to-all(bf16[4,144,256]{2,1,0:T(8,128)(2,1)} %gate.3), channel_id=1, replica_groups=mesh['section'=4,'seq_0'=4,'seq_1'=2,'tp_hi'=8,'tp_lo'=4] {'tp_lo'}, dimensions={0} | all-to-all | bytes 589824 | tf_op jit(solution)/shard_map/all_to_all | solution.py:19
  380.3 3.9 close.3
  384.2 40.3 %all_to_all.59 = bf16[8,128,128]{2,1,0:T(8,128)(2,1)S(1)} all-to-all(bf16[8,128,128]{2,1,0:T(8,128)(2,1)} %close.3), channel_id=1, replica_groups=mesh['section'=4,'seq_0'=4,'seq_1'=2,'tp_hi'=8,'tp_lo'=4] {'tp_hi'}, dimensions={0} | all-to-all | bytes 524288 | tf_op jit(solution)/shard_map/all_to_all | solution.py:19
  (131 shorter events, 83.5 us)
Async XLA Ops:
  0.0 31.2 %copy-start = (bf16[1,256,4096]{2,1,0:T(8,128)(2,1)S(1)}, bf16[1,256,4096]{2,1,0:T(8,128)(2,1)}, u32[]{:S(2)}) copy-start(bf16[1,256,4096]{2,1,0:T(8,128)(2,1)} %param.21) | copy-start | bytes 6291460
  2.0 39.4 %copy-start.23 = (s32[1,4]{1,0:T(1,128)S(1)}, s32[1,4]{1,0:T(1,128)}, u32[]{:S(2)}) copy-start(s32[1,4]{1,0:T(1,128)} %param.17) | copy-start | bytes 52
  2.8 71.2 %all-to-all-start = ((bf16[8,192,128]{2,1,0:T(8,128)(2,1)}), bf16[8,192,128]{2,1,0:T(8,128)(2,1)S(1)}, u32[]{:S(2)}, u32[]{:S(2)}) async-start(bf16[8,192,128]{2,1,0:T(8,128)(2,1)} %pad_maximum_fusion), calls=%async_computation | async-start | bytes 786432 | tf_op jit(solution)/shard_map/all_to_all | solution.py:19
  32.2 32.1 %collective-permute-start.7 = (bf16[32,1024]{1,0:T(8,128)(2,1)S(1)}, bf16[32,1024]{1,0:T(8,128)(2,1)S(1)}, u32[]{:S(2)}, u32[]{:S(2)}) collective-permute-start(bf16[32,1024]{1,0:T(8,128)(2,1)S(1)} %get-tuple-element.69), channel_id=1, source_target_pairs={{0,3},{1,0},{2,1},{3,2},{4,7},{5,4},{6,5},{7,6},{8,11},{9,8},{10,9... | collective-permute-start | bytes 196616 | tf_op jit(solution)/shard_map/ppermute | solution.py:317
  36.1 35.6 %collective-permute-start.8 = (bf16[32,1024]{1,0:T(8,128)(2,1)S(1)}, bf16[32,1024]{1,0:T(8,128)(2,1)S(1)}, u32[]{:S(2)}, u32[]{:S(2)}) collective-permute-start(bf16[32,1024]{1,0:T(8,128)(2,1)S(1)} %get-tuple-element.68), channel_id=1, source_target_pairs={{0,2},{1,3},{2,0},{3,1},{4,6},{5,7},{6,4},{7,5},{8,10},{9,11},{10,... | collective-permute-start | bytes 196616 | tf_op jit(solution)/shard_map/ppermute | solution.py:317
  38.5 33.7 %collective-permute-start.9 = (bf16[32,1024]{1,0:T(8,128)(2,1)S(1)}, bf16[32,1024]{1,0:T(8,128)(2,1)S(1)}, u32[]{:S(2)}, u32[]{:S(2)}) collective-permute-start(bf16[32,1024]{1,0:T(8,128)(2,1)S(1)} %get-tuple-element.66), channel_id=1, source_target_pairs={{0,1},{1,2},{2,3},{3,0},{4,5},{5,6},{6,7},{7,4},{8,9},{9,10},{10,1... | collective-permute-start | bytes 196616 | tf_op jit(solution)/shard_map/ppermute | solution.py:317
  75.7 20.9 %all-to-all-start.1 = ((bf16[4,8,4,16,128]{4,3,2,1,0:T(8,128)(2,1)}), bf16[4,8,4,16,128]{4,3,2,1,0:T(8,128)(2,1)S(1)}, u32[]{:S(2)}, u32[]{:S(2)}) async-start(bf16[4,8,4,16,128]{4,3,2,1,0:T(8,128)(2,1)} %broadcast_in_dim.32), calls=%async_computation.1 | async-start | bytes 1048576 | tf_op jit(solution)/shard_map/all_to_all | solution.py:19
  81.3 32.4 %collective-permute-start.1 = (bf16[8,64,128]{2,1,0:T(8,128)(2,1)}, bf16[8,64,128]{2,1,0:T(8,128)(2,1)}, u32[]{:S(2)}, u32[]{:S(2)}) collective-permute-start(bf16[8,64,128]{2,1,0:T(8,128)(2,1)} %get-tuple-element.63), channel_id=1, source_target_pairs={{0,2},{1,3},{2,4},{3,5},{4,6},{5,7},{6,8},{7,9},{8,10},{9,11},{10,... | collective-permute-start | bytes 393224 | tf_op jit(solution)/shard_map/ppermute | solution.py:28
  96.6 26.5 %copy-start.1 = (bf16[4,8,4,16,128]{4,3,2,1,0:T(8,128)(2,1)}, bf16[4,8,4,16,128]{4,3,2,1,0:T(8,128)(2,1)S(1)}, u32[]{:S(2)}) copy-start(bf16[4,8,4,16,128]{4,3,2,1,0:T(8,128)(2,1)S(1)} %all-to-all-done.1.same) | copy-start | bytes 1572868
  96.6 28.5 %collective-permute-start.4 = (bf16[4,8,4,16,128]{4,3,2,1,0:T(8,128)(2,1)S(1)}, bf16[4,8,4,16,128]{4,3,2,1,0:T(8,128)(2,1)S(1)}, u32[]{:S(2)}, u32[]{:S(2)}) collective-permute-start(bf16[4,8,4,16,128]{4,3,2,1,0:T(8,128)(2,1)S(1)} %all-to-all-done.1.same), channel_id=1, source_target_pairs={{0,32},{32,0},{1,33},{33,1},{2,34},{34,2},{3,35},{35,3},{4,36},{36... | collective-permute-start | bytes 1572872 | tf_op jit(solution)/shard_map/ppermute | solution.py:304
  100.8 24.3 %collective-permute-start = (bf16[8,128,128]{2,1,0:T(8,128)(2,1)}, bf16[8,128,128]{2,1,0:T(8,128)(2,1)}, u32[]{:S(2)}, u32[]{:S(2)}) collective-permute-start(bf16[8,128,128]{2,1,0:T(8,128)(2,1)} %slice.26.far), channel_id=1, source_target_pairs={{0,31},{1,0},{2,1},{3,2},{4,3},{5,4},{6,5},{7,6},{8,7},{9,8},{10,9... | collective-permute-start | bytes 786440 | tf_op jit(solution)/shard_map/ppermute | solution.py:28
  102.8 22.3 %collective-permute-start.3 = (bf16[8,128,128]{2,1,0:T(8,128)(2,1)}, bf16[8,128,128]{2,1,0:T(8,128)(2,1)}, u32[]{:S(2)}, u32[]{:S(2)}) collective-permute-start(bf16[8,128,128]{2,1,0:T(8,128)(2,1)} %slice.26.far), channel_id=1, source_target_pairs={{0,1},{1,2},{2,3},{3,4},{4,5},{5,6},{6,7},{7,8},{8,9},{9,10},{10,1... | collective-permute-start | bytes 786440 | tf_op jit(solution)/shard_map/ppermute | solution.py:28
  108.6 37.5 %collective-permute-start.10 = (bf16[4,32,1024]{2,1,0:T(8,128)(2,1)}, bf16[4,32,1024]{2,1,0:T(8,128)(2,1)S(1)}, u32[]{:S(2)}, u32[]{:S(2)}) collective-permute-start(bf16[4,32,1024]{2,1,0:T(8,128)(2,1)} %get-tuple-element.58), channel_id=1, source_target_pairs={{0,192},{64,0},{128,64},{192,128},{1,193},{65,1},{129,65},{193,129... | collective-permute-start | bytes 786440 | tf_op jit(solution)/shard_map/ppermute | solution.py:317
  113.7 11.4 %collective-permute-start.2 = (bf16[8,64,128]{2,1,0:T(8,128)(2,1)}, bf16[8,64,128]{2,1,0:T(8,128)(2,1)S(1)}, u32[]{:S(2)}, u32[]{:S(2)}) collective-permute-start(bf16[8,64,128]{2,1,0:T(8,128)(2,1)} %get-tuple-element.62), channel_id=1, source_target_pairs={{0,30},{1,31},{2,0},{3,1},{4,2},{5,3},{6,4},{7,5},{8,6},{9,7},{10,... | collective-permute-start | bytes 393224 | tf_op jit(solution)/shard_map/ppermute | solution.py:28
  134.9 22.0 %all-to-all-start.2 = ((bf16[4,128,128]{2,1,0:T(8,128)(2,1)}), bf16[4,128,128]{2,1,0:T(8,128)(2,1)S(1)}, u32[]{:S(2)}, u32[]{:S(2)}) async-start(bf16[4,128,128]{2,1,0:T(8,128)(2,1)} %get-tuple-element.31), calls=%async_computation.2 | async-start | bytes 262144 | tf_op jit(solution)/shard_map/all_to_all | solution.py:19
  140.0 12.3 %collective-permute-start.11 = (bf16[4,32,1024]{2,1,0:T(8,128)(2,1)}, bf16[4,32,1024]{2,1,0:T(8,128)(2,1)S(1)}, u32[]{:S(2)}, u32[]{:S(2)}) collective-permute-start(bf16[4,32,1024]{2,1,0:T(8,128)(2,1)} %get-tuple-element.58), channel_id=1, source_target_pairs={{0,128},{64,192},{128,0},{192,64},{1,129},{65,193},{129,1},{193,65... | collective-permute-start | bytes 786440 | tf_op jit(solution)/shard_map/ppermute | solution.py:317
  144.1 12.1 %collective-permute-start.12 = (bf16[4,32,1024]{2,1,0:T(8,128)(2,1)}, bf16[4,32,1024]{2,1,0:T(8,128)(2,1)S(1)}, u32[]{:S(2)}, u32[]{:S(2)}) collective-permute-start(bf16[4,32,1024]{2,1,0:T(8,128)(2,1)} %get-tuple-element.58), channel_id=1, source_target_pairs={{0,64},{64,128},{128,192},{192,0},{1,65},{65,129},{129,193},{193,1... | collective-permute-start | bytes 786440 | tf_op jit(solution)/shard_map/ppermute | solution.py:317
  153.1 3.9 collective-permute-start.5
  160.1 13.3 %all-to-all-start.3 = ((bf16[4,272,256]{2,1,0:T(8,128)(2,1)}), bf16[4,272,256]{2,1,0:T(8,128)(2,1)S(1)}, u32[]{:S(2)}, u32[]{:S(2)}) async-start(bf16[4,272,256]{2,1,0:T(8,128)(2,1)} %get-tuple-element.36), calls=%async_computation.3 | async-start | bytes 1114112 | tf_op jit(solution)/shard_map/all_to_all | solution.py:19
  176.2 3.4 collective-permute-start.6
  182.6 15.7 %all-to-all-start.4 = ((bf16[4,144,256]{2,1,0:T(8,128)(2,1)}), bf16[4,144,256]{2,1,0:T(8,128)(2,1)S(1)}, u32[]{:S(2)}, u32[]{:S(2)}) async-start(bf16[4,144,256]{2,1,0:T(8,128)(2,1)} %gate.2), calls=%async_computation.4 | async-start | bytes 589824 | tf_op jit(solution)/shard_map/all_to_all | solution.py:19
  190.4 4.8 %collective-permute-start.13 = (bf16[4,4,32,1024]{3,2,1,0:T(8,128)(2,1)}, bf16[4,4,32,1024]{3,2,1,0:T(8,128)(2,1)S(1)}, u32[]{:S(2)}, u32[]{:S(2)}) collective-permute-start(bf16[4,4,32,1024]{3,2,1,0:T(8,128)(2,1)} %constant_dynamic-slice_fusion), channel_id=1, source_target_pairs={{0,32},{32,0},{1,33},{33,1},{2,34},{34,2},{3,35},{35,3},{4,36},{36... | collective-permute-start | bytes 3145736 | tf_op jit(solution)/shard_map/ppermute | solution.py:304
  198.3 47.3 %copy-start.15 = (bf16[1,128,128]{2,1,0:T(8,128)(2,1)S(1)}, bf16[1,128,128]{2,1,0:T(8,128)(2,1)}, u32[]{:S(2)}) copy-start(bf16[1,128,128]{2,1,0:T(8,128)(2,1)} %param.11) | copy-start | bytes 98308
  198.3 53.1 %copy-start.18 = (bf16[128,128]{1,0:T(8,128)(2,1)S(1)}, bf16[128,128]{1,0:T(8,128)(2,1)}, u32[]{:S(2)}) copy-start(bf16[128,128]{1,0:T(8,128)(2,1)} %param.12) | copy-start | bytes 98308
  245.6 5.8 %collective-permute-start.14 = (bf16[128,128]{1,0:T(8,128)(2,1)S(1)}, bf16[128,128]{1,0:T(8,128)(2,1)S(1)}, u32[]{:S(2)}, u32[]{:S(2)}) collective-permute-start(bf16[128,128]{1,0:T(8,128)(2,1)S(1)} %add_convert_fusion.1), channel_id=1, source_target_pairs={{0,256},{256,512},{512,768},{1,257},{257,513},{513,769},{2,258},{2... | collective-permute-start | bytes 98312 | tf_op jit(solution)/shard_map/ppermute | solution.py:450
  302.9 19.1 %collective-permute-start.15 = (bf16[8,128,128]{2,1,0:T(8,128)(2,1)S(1)}, bf16[8,128,128]{2,1,0:T(8,128)(2,1)S(1)}, u32[]{:S(2)}, u32[]{:S(2)}) collective-permute-start(bf16[8,128,128]{2,1,0:T(8,128)(2,1)S(1)} %all_to_all.56.far), channel_id=1, source_target_pairs={{0,31},{1,0},{2,1},{3,2},{4,3},{5,4},{6,5},{7,6},{8,7},{9,8},{10,9... | collective-permute-start | bytes 786440 | tf_op jit(solution)/shard_map/ppermute | solution.py:28
  304.8 17.2 %collective-permute-start.18 = (bf16[8,128,128]{2,1,0:T(8,128)(2,1)S(1)}, bf16[8,128,128]{2,1,0:T(8,128)(2,1)S(1)}, u32[]{:S(2)}, u32[]{:S(2)}) collective-permute-start(bf16[8,128,128]{2,1,0:T(8,128)(2,1)S(1)} %all_to_all.56.far), channel_id=1, source_target_pairs={{0,1},{1,2},{2,3},{3,4},{4,5},{5,6},{6,7},{7,8},{8,9},{9,10},{10,1... | collective-permute-start | bytes 786440 | tf_op jit(solution)/shard_map/ppermute | solution.py:28
  308.8 13.2 %collective-permute-start.16 = (bf16[8,64,128]{2,1,0:T(8,128)(2,1)S(1)}, bf16[8,64,128]{2,1,0:T(8,128)(2,1)S(1)}, u32[]{:S(2)}, u32[]{:S(2)}) collective-permute-start(bf16[8,64,128]{2,1,0:T(8,128)(2,1)S(1)} %get-tuple-element.65), channel_id=1, source_target_pairs={{0,2},{1,3},{2,4},{3,5},{4,6},{5,7},{6,8},{7,9},{8,10},{9,11},{10,... | collective-permute-start | bytes 393224 | tf_op jit(solution)/shard_map/ppermute | solution.py:28
  313.1 8.9 %collective-permute-start.17 = (bf16[8,64,128]{2,1,0:T(8,128)(2,1)S(1)}, bf16[8,64,128]{2,1,0:T(8,128)(2,1)S(1)}, u32[]{:S(2)}, u32[]{:S(2)}) collective-permute-start(bf16[8,64,128]{2,1,0:T(8,128)(2,1)S(1)} %get-tuple-element.64), channel_id=1, source_target_pairs={{0,30},{1,31},{2,0},{3,1},{4,2},{5,3},{6,4},{7,5},{8,6},{9,7},{10,... | collective-permute-start | bytes 393224 | tf_op jit(solution)/shard_map/ppermute | solution.py:28
  332.5 9.2 %all-to-all-start.7 = ((bf16[4,128,128]{2,1,0:T(8,128)(2,1)}), bf16[4,128,128]{2,1,0:T(8,128)(2,1)S(1)}, u32[]{:S(2)}, u32[]{:S(2)}) async-start(bf16[4,128,128]{2,1,0:T(8,128)(2,1)} %get-tuple-element.44), calls=%async_computation.7 | async-start | bytes 262144 | tf_op jit(solution)/shard_map/all_to_all | solution.py:19
  335.8 3.3 collective-permute-start.19
  359.3 3.4 collective-permute-start.20
  (19 other events, 88.1 us)
